TPU v7x, 512 devices: a whole 4x4x16 slice. The times are simulated.
512 devices in a mesh: user: 64 (over y, z), item: 8 (over x, core).
Axes of the slice: x: 4, y: 4, z: 16, core: 2. Of those that a mesh axis runs over, the one named last changes fastest.
Arguments:
- user_factors: bfloat16 [65536, 256], P('user'), may hold values from -0.3984375 to 0.3984375
- item_panels: float32 [524288, 256], P(('user', 'item')), may hold values from -6 to 6
- ratings: bfloat16 [3, 1536, 1024, 128], P(None, 'user', 'item'), may hold values from -6 to 6
- tile_ids: int32 [3, 1536, 8], P(None, 'user', 'item'), may hold values from 0 to 63, as said below
- tile_count: int32 [3, 64, 8], P(None, 'user', 'item'), may hold values from 6 to 24, as said below
Outputs:
- panels_out: float32 [524288, 256], P(('user', 'item'))
- user_grad: float32 [65536, 256], P(('user', 'item'))
Inputs may be any that keep to these rules, and one draw needn't show every extreme that they name: `tile_ids`: the first 24 entries of each user block's list for a group and step are distinct tiles of the block. `tile_count`: in every step some user block and group has all 24 slots live.
All inputs are finite; a program needn't handle non-finite values.
Results may differ from a plain program's by a relative error of at most 0.0013.
Values sent between devices are 32-bit elements; how exact they have to be, the bound alone decides.
No kernel may reach another device: no remote copies, remote signals or barrier semaphores. Data moves between devices by JAX's collectives and lax.ppermute only.
A program may use at most 64 MiB of HBM per device.

v0:
```python
import jax
import jax.numpy as jnp
from jax import lax
from jax.sharding import PartitionSpec as P

R = 256
TILE = 128
STEPS = 3


learn_rate = 0.05
weight_decay = 0.02
user_scale = 1.0 / 64.0


def passed_along(value, axis, steps):
    count = lax.axis_size(axis)
    pairs = [(source, (source + steps) % count) for source in range(count)]
    return lax.ppermute(value, axis, pairs)


def padded_update(user_block, item_block, rating_tiles, tile_list, live_count):
    row_tiles = user_block.shape[0] // TILE
    col_tiles = item_block.shape[0] // TILE
    row_index = tile_list // col_tiles
    col_index = tile_list % col_tiles
    user_tiles = user_block.reshape(row_tiles, TILE, R)[row_index]
    item_tiles = item_block.astype(jnp.bfloat16).reshape(col_tiles, TILE, R)[col_index]
    predicted = jnp.einsum(
        "kir,kjr->kij", user_tiles, item_tiles, preferred_element_type=jnp.float32
    )
    live_mask = (jnp.arange(tile_list.shape[0]) < live_count).astype(jnp.float32)
    residual = ((predicted - rating_tiles.astype(jnp.float32)) * live_mask[:, None, None]).astype(
        jnp.bfloat16
    )
    item_parts = jnp.einsum(
        "kij,kir->kjr", residual, user_tiles, preferred_element_type=jnp.float32
    )
    user_parts = jnp.einsum(
        "kij,kjr->kir", residual, item_tiles, preferred_element_type=jnp.float32
    )
    col_pick = (col_index[:, None] == jnp.arange(col_tiles)[None, :]).astype(jnp.float32)
    row_pick = (row_index[:, None] == jnp.arange(row_tiles)[None, :]).astype(jnp.float32)
    item_grad = jnp.einsum(
        "kc,kjr->cjr", col_pick, item_parts, precision=lax.Precision.HIGHEST
    ).reshape(-1, R)
    user_grad = jnp.einsum(
        "ka,kir->air", row_pick, user_parts, precision=lax.Precision.HIGHEST
    ).reshape(-1, R)
    return (item_grad, user_grad)


def shards(user_factors, item_panels, ratings, tile_ids, tile_count):
    held_panel = item_panels
    user_rows = user_factors.shape[0]
    total_grad = jnp.zeros((user_rows, R), jnp.float32)
    for step_index in range(STEPS):
        if step_index > 0:
            held_panel = passed_along(held_panel, "user", 1)
        tile_list = tile_ids[step_index, :, 0]
        live_count = tile_count[step_index, 0, 0]
        rating_tiles = ratings[step_index]
        item_grad, user_grad = padded_update(
            user_factors, held_panel, rating_tiles, tile_list, live_count
        )
        held_panel = held_panel - learn_rate * (item_grad + weight_decay * held_panel)
        user_part = user_scale * user_grad
        total_grad = total_grad + user_part
    share_grad = lax.psum_scatter(total_grad, "item", scatter_dimension=0, tiled=True)
    return (held_panel, share_grad)


def solution(mesh):
    in_specs = (
        P("user", None),
        P(("user", "item"), None),
        P(None, "user", "item", None),
        P(None, "user", "item"),
        P(None, "user", "item"),
    )
    out_specs = (P(("user", "item"), None), P(("user", "item"), None))
    return jax.shard_map(shards, mesh=mesh, in_specs=in_specs, out_specs=out_specs, check_vma=False)
```

profile of v0, /device:TPU:1, one launch (start us, length us, event | category | flops | bytes accessed | tf_op | source)
XLA Modules:
  0.0 153.8 jit_solution(9428702966692573336)
XLA Ops:
  7.2 0.7 fusion.56
  8.0 0.7 and_select_fusion
  8.7 0.7 fusion.54
  9.4 1.3 convert_element_type.63
  12.0 1.8 %gather_fusion = bf16[24,128,256]{2,1,0:T(8,128)(2,1)} fusion(bf16[8,128,256]{2,1,0:T(8,128)(2,1)S(1)} %bitcast.161, s32[1024]{0:T(1024)S(1)} %get-tuple-element.27), kind=kCustom, calls=%fused_computation | custom fusion | bytes 3145824 | tf_op jit(solution)/shard_map/gather | solution.py:27
  14.5 2.8 %fusion.17 = bf16[24,128,128]{2,1,0:T(8,128)(2,1)S(1)} fusion(bf16[24,128,256]{2,1,0:T(8,128)(2,1)} %gather_fusion, bf16[24,128,256]{2,1,0:T(8,128)(2,1)S(1)} %gather_fusion.1, f32[24]{0:T(128)S(1)} %compare_convert_fusion.2, bf16[3,24,128,128]{3,2,1,0:T(8,128)(2,1)} %param.7), kind=kOutput, calls=%fused_computation.26 | convolution fusion | flops 202899456 | bytes 4718688 | tf_op jit(solution)/shard_map/kir,kjr->kij/dot_general | solution.py:29
  17.9 2.9 %fusion.10 = f32[8,128,256]{2,0,1:T(8,128)S(1)} fusion(f32[24,128,256]{2,1,0:T(8,128)S(1)} %fusion.58, s32[24]{0:T(128)S(1)} %and_select_fusion.11), kind=kOutput, calls=%fused_computation.16 | convolution fusion | flops 75497664 | bytes 4194400 | tf_op jit(solution)/shard_map/kc,kjr->cjr/dot_general | solution.py:44
  21.2 0.9 copy-done.9
  22.1 1.1 fusion.32
  23.2 4.4 %collective-permute-start = (f32[1024,256]{1,0:T(8,128)}, f32[1024,256]{1,0:T(8,128)}, u32[]{:S(2)}, u32[]{:S(2)}) collective-permute-start(f32[1024,256]{1,0:T(8,128)} %fusion.32), channel_id=1, source_target_pairs={{0,8},{8,16},{16,24},{24,32},{32,40},{40,48},{48,56},{56,64},{64,7... | collective-permute-start | bytes 3145736 | tf_op jit(solution)/shard_map/ppermute | solution.py:19
  27.6 1.8 %gather_fusion.2 = bf16[24,128,256]{2,1,0:T(8,128)(2,1)} fusion(bf16[8,128,256]{2,1,0:T(8,128)(2,1)S(1)} %bitcast.162, s32[1024]{0:T(1024)S(1)} %get-tuple-element.26), kind=kCustom, calls=%fused_computation.2 | custom fusion | bytes 3145824 | tf_op jit(solution)/shard_map/gather | solution.py:27
  31.3 29.4 %collective-permute-done = f32[1024,256]{1,0:T(8,128)} collective-permute-done((f32[1024,256]{1,0:T(8,128)}, f32[1024,256]{1,0:T(8,128)}, u32[]{:S(2)}, u32[]{:S(2)}) %collective-permute-start) | collective-permute-done | bytes 1048608 | tf_op jit(solution)/shard_map/ppermute | solution.py:19
  60.7 1.3 convert_element_type.68
  62.0 1.9 %gather_fusion.3 = bf16[24,128,256]{2,1,0:T(8,128)(2,1)} fusion(bf16[8,128,256]{2,1,0:T(8,128)(2,1)S(1)} %bitcast.165, s32[1024]{0:T(1024)S(1)} %pad_clamp_fusion.2), kind=kCustom, calls=%fused_computation.3 | custom fusion | bytes 3145824 | tf_op jit(solution)/shard_map/gather | solution.py:28
  63.9 2.8 %fusion.15 = bf16[24,128,128]{2,1,0:T(8,128)(2,1)S(1)} fusion(bf16[24,128,256]{2,1,0:T(8,128)(2,1)} %gather_fusion.2, bf16[24,128,256]{2,1,0:T(8,128)(2,1)} %gather_fusion.3, f32[24]{0:T(128)S(1)} %compare_convert_fusion.1, bf16[3,24,128,128]{3,2,1,0:T(8,128)(2,1)} %param.7), kind=kOutput, calls=%fused_computation.23 | convolution fusion | flops 202899456 | bytes 4718688 | tf_op jit(solution)/shard_map/kir,kjr->kij/dot_general | solution.py:29
  67.3 2.9 %fusion.8 = f32[8,128,256]{2,0,1:T(8,128)S(1)} fusion(f32[24,128,256]{2,1,0:T(8,128)S(1)} %fusion.59, s32[24]{0:T(128)S(1)} %get-tuple-element.29), kind=kOutput, calls=%fused_computation.14 | convolution fusion | flops 75497664 | bytes 4194400 | tf_op jit(solution)/shard_map/kc,kjr->cjr/dot_general | solution.py:44
  70.6 1.5 fusion.30
  72.1 2.2 %collective-permute-start.1 = (f32[1024,256]{1,0:T(8,128)S(1)}, f32[1024,256]{1,0:T(8,128)S(1)}, u32[]{:S(2)}, u32[]{:S(2)}) collective-permute-start(f32[1024,256]{1,0:T(8,128)S(1)} %fusion.30), channel_id=1, source_target_pairs={{0,8},{8,16},{16,24},{24,32},{32,40},{40,48},{48,56},{56,64},{64,7... | collective-permute-start | bytes 3145736 | tf_op jit(solution)/shard_map/ppermute | solution.py:19
  74.3 2.2 %fusion.61 = f32[24,128,256]{2,1,0:T(8,128)} fusion(bf16[24,128,128]{2,1,0:T(8,128)(2,1)S(1)} %fusion.17, bf16[24,128,256]{2,1,0:T(8,128)(2,1)S(1)} %copy-done.2), kind=kOutput, calls=%fused_computation.118 | convolution fusion | flops 201326592 | bytes 5505024 | tf_op jit(solution)/shard_map/kij,kjr->kir/dot_general | solution.py:39
  77.1 3.9 %fusion.2 = f32[8,128,256]{2,0,1:T(8,128)} fusion(f32[24,128,256]{2,1,0:T(8,128)S(1)} %fusion.62, s32[24]{0:T(128)S(1)} %get-tuple-element.14), kind=kOutput, calls=%fused_computation.8 | convolution fusion | flops 75497664 | bytes 4194400 | tf_op jit(solution)/shard_map/ka,kir->air/dot_general | solution.py:47
  81.0 19.9 %collective-permute-done.1 = f32[1024,256]{1,0:T(8,128)S(1)} collective-permute-done((f32[1024,256]{1,0:T(8,128)S(1)}, f32[1024,256]{1,0:T(8,128)S(1)}, u32[]{:S(2)}, u32[]{:S(2)}) %collective-permute-start.1) | collective-permute-done | bytes 1048608 | tf_op jit(solution)/shard_map/ppermute | solution.py:19
  100.9 1.0 copy-done.10
  101.9 1.9 %gather_fusion.5 = bf16[24,128,256]{2,1,0:T(8,128)(2,1)} fusion(bf16[8,128,256]{2,1,0:T(8,128)(2,1)S(1)} %bitcast.166, s32[1024]{0:T(1024)S(1)} %pad_clamp_fusion), kind=kCustom, calls=%fused_computation.5 | custom fusion | bytes 3145824 | tf_op jit(solution)/shard_map/gather | solution.py:28
  103.8 2.3 %fusion.13 = bf16[24,128,128]{2,1,0:T(8,128)(2,1)S(1)} fusion(bf16[24,128,256]{2,1,0:T(8,128)(2,1)S(1)} %gather_fusion.4, bf16[24,128,256]{2,1,0:T(8,128)(2,1)} %gather_fusion.5, f32[24]{0:T(128)S(1)} %compare_convert_fusion, bf16[3,24,128,128]{3,2,1,0:T(8,128)(2,1)} %param.7), kind=kOutput, calls=%fused_computation.20 | convolution fusion | flops 202899456 | bytes 4718688 | tf_op jit(solution)/shard_map/kir,kjr->kij/dot_general | solution.py:29
  106.7 2.9 %fusion = f32[8,128,256]{2,0,1:T(8,128)S(1)} fusion(f32[24,128,256]{2,1,0:T(8,128)S(1)} %fusion.63, s32[24]{0:T(128)S(1)} %get-tuple-element.6), kind=kOutput, calls=%fused_computation.6 | convolution fusion | flops 75497664 | bytes 4194400 | tf_op jit(solution)/shard_map/ka,kir->air/dot_general | solution.py:47
  109.6 3.0 %fusion.24 = f32[8,128,256]{2,0,1:T(8,128)S(1)} fusion(f32[8,128,256]{2,0,1:T(8,128)S(1)} %fusion, f32[8,128,256]{2,0,1:T(8,128)S(1)} %copy-done.8, f32[24,128,256]{2,1,0:T(8,128)S(1)} %copy-done.7, s32[24]{0:T(128)S(1)} %get-tuple-element.16), kind=kOutput, calls=%fused_computation.29 | convolution fusion | flops 76284096 | bytes 6291552 | tf_op jit(solution)/shard_map/ka,kir->air/dot_general | solution.py:47
  112.6 1.3 copy.10
  114.0 0.9 fusion.60
  114.8 2.9 %fusion.6 = f32[8,128,256]{2,0,1:T(8,128)S(1)} fusion(f32[24,128,256]{2,1,0:T(8,128)S(1)} %fusion.60, s32[24]{0:T(128)S(1)} %get-tuple-element.28), kind=kOutput, calls=%fused_computation.12 | convolution fusion | flops 75497664 | bytes 4194400 | tf_op jit(solution)/shard_map/kc,kjr->cjr/dot_general | solution.py:44
  118.1 0.9 copy-done.11
  119.0 1.1 fusion.28
  120.1 26.8 %reduce-scatter.2.cloned.1.call-done = f32[128,256]{1,0:T(8,128)} async-done(((f32[1024,256]{1,0:T(8,128)}), f32[128,256]{1,0:T(8,128)}) %reduce-scatter.2.cloned.1.call-update) | async-done | bytes 131088 | tf_op jit(solution)/shard_map/reduce_scatter | solution.py:69
  (49 shorter events, 7.4 us)
Async XLA Ops:
  7.2 4.8 %copy-start = (bf16[1024,256]{1,0:T(8,128)(2,1)S(1)}, bf16[1024,256]{1,0:T(8,128)(2,1)}, u32[]{:S(2)}) copy-start(bf16[1024,256]{1,0:T(8,128)(2,1)} %param.5) | copy-start | bytes 1572868
  7.2 4.7 %copy-start.12 = (s32[3,24,1]{1,2,0:T(1,128)S(1)}, s32[3,24,1]{1,2,0:T(1,128)}, u32[]{:S(2)}) copy-start(s32[3,24,1]{1,2,0:T(1,128)} %param.8) | copy-start | bytes 868
  7.2 3.5 %copy-start.13 = (s32[3,1,1]{0,2,1:T(1,128)S(1)}, s32[3,1,1]{0,2,1:T(1,128)}, u32[]{:S(2)}) copy-start(s32[3,1,1]{0,2,1:T(1,128)} %param.9) | copy-start | bytes 40
  7.2 139.8 %reduce-scatter.2.cloned.1.call-start = ((), (), s32[]{:S(2)}) async-start(), calls=%async_computation.1 | async-start | bytes 1179648 | tf_op jit(solution)/shard_map/reduce_scatter | solution.py:69
  14.4 2.8 %copy-start.1 = (bf16[24,128,256]{2,1,0:T(8,128)(2,1)}, bf16[24,128,256]{2,1,0:T(8,128)(2,1)S(1)}, u32[]{:S(2)}) copy-start(bf16[24,128,256]{2,1,0:T(8,128)(2,1)S(1)} %gather_fusion.1) | copy-start | bytes 4718596
  14.5 2.8 %copy-start.5 = (bf16[24,128,256]{2,1,0:T(8,128)(2,1)S(1)}, bf16[24,128,256]{2,1,0:T(8,128)(2,1)}, u32[]{:S(2)}) copy-start(bf16[24,128,256]{2,1,0:T(8,128)(2,1)} %gather_fusion) | copy-start | bytes 4718596
  20.8 1.2 copy-start.9
  23.2 37.5 %collective-permute-start = (f32[1024,256]{1,0:T(8,128)}, f32[1024,256]{1,0:T(8,128)}, u32[]{:S(2)}, u32[]{:S(2)}) collective-permute-start(f32[1024,256]{1,0:T(8,128)} %fusion.32), channel_id=1, source_target_pairs={{0,8},{8,16},{16,24},{24,32},{32,40},{40,48},{48,56},{56,64},{64,7... | collective-permute-start | bytes 3145736 | tf_op jit(solution)/shard_map/ppermute | solution.py:19
  63.9 2.8 %copy-start.3 = (bf16[24,128,256]{2,1,0:T(8,128)(2,1)S(1)}, bf16[24,128,256]{2,1,0:T(8,128)(2,1)}, u32[]{:S(2)}) copy-start(bf16[24,128,256]{2,1,0:T(8,128)(2,1)} %gather_fusion.2) | copy-start | bytes 4718596
  70.6 3.8 %copy-start.2 = (bf16[24,128,256]{2,1,0:T(8,128)(2,1)S(1)}, bf16[24,128,256]{2,1,0:T(8,128)(2,1)}, u32[]{:S(2)}) copy-start(bf16[24,128,256]{2,1,0:T(8,128)(2,1)} %copy-done.1) | copy-start | bytes 4718596
  72.1 4.5 %copy-start.4 = (bf16[24,128,256]{2,1,0:T(8,128)(2,1)S(1)}, bf16[24,128,256]{2,1,0:T(8,128)(2,1)}, u32[]{:S(2)}) copy-start(bf16[24,128,256]{2,1,0:T(8,128)(2,1)} %gather_fusion.3) | copy-start | bytes 4718596
  72.1 28.8 %collective-permute-start.1 = (f32[1024,256]{1,0:T(8,128)S(1)}, f32[1024,256]{1,0:T(8,128)S(1)}, u32[]{:S(2)}, u32[]{:S(2)}) collective-permute-start(f32[1024,256]{1,0:T(8,128)S(1)} %fusion.30), channel_id=1, source_target_pairs={{0,8},{8,16},{16,24},{24,32},{32,40},{40,48},{48,56},{56,64},{64,7... | collective-permute-start | bytes 3145736 | tf_op jit(solution)/shard_map/ppermute | solution.py:19
  100.9 1.0 copy-start.10
  103.8 2.3 %copy-start.6 = (bf16[24,128,256]{2,1,0:T(8,128)(2,1)S(1)}, bf16[24,128,256]{2,1,0:T(8,128)(2,1)}, u32[]{:S(2)}) copy-start(bf16[24,128,256]{2,1,0:T(8,128)(2,1)} %gather_fusion.5) | copy-start | bytes 4718596
  106.7 2.9 %copy-start.7 = (f32[24,128,256]{2,1,0:T(8,128)S(1)}, f32[24,128,256]{2,1,0:T(8,128)}, u32[]{:S(2)}) copy-start(f32[24,128,256]{2,1,0:T(8,128)} %fusion.61) | copy-start | bytes 9437188
  106.7 2.9 %copy-start.8 = (f32[8,128,256]{2,0,1:T(8,128)S(1)}, f32[8,128,256]{2,0,1:T(8,128)}, u32[]{:S(2)}) copy-start(f32[8,128,256]{2,0,1:T(8,128)} %fusion.2) | copy-start | bytes 3145732
  117.7 1.2 copy-start.11
Sparse Core Ops, SparseCore 0:
  114.1 32.8 reduce-scatter.1
where the time goes:
time: 155 us; the launch traced here: 154 us
  waiting for transfers between devices  76.2 us (49%)
  matrix products  31.8 us (21%)
  local copies, waits for them, and re-layouts  14.4 us (9%)
  between operations  14.4 us (9%)
  other arithmetic  10.4 us (7%)
  starting transfers between devices  6.62 us (4%)
    ppermute x2, waiting for transfers between devices, passed_along(): return lax.ppermute(value, axis, pairs)  49.3 us
    reduce_scatter x1, waiting for transfers between devices, shards(): lax.psum_scatter(total_grad, 'item', scatter_dimension=0, tiled=True)  26.8 us
    dot_general x3, matrix products, padded_update(): jnp.einsum('ka,kir->air', row_pick, user_parts, precision=lax.Precision.H...  9.76 us
    dot_general x3, matrix products, padded_update(): jnp.einsum('kc,kjr->cjr', col_pick, item_parts, precision=lax.Precision.H...  8.7 us
    dot_general x3, matrix products, padded_update(): jnp.einsum('kir,kjr->kij', user_tiles, item_tiles, preferred_element_type...  7.85 us
    ppermute x2, starting transfers between devices, passed_along(): return lax.ppermute(value, axis, pairs)  6.59 us
    gather x3, local copies, waits for them, and re-layouts, padded_update(): item_block.astype(jnp.bfloat16).reshape(col_tiles, TILE, R)[col_index]  4.37 us
    gather x3, local copies, waits for them, and re-layouts, padded_update(): user_tiles = user_block.reshape(row_tiles, TILE, R)[row_index]  4.31 us
  transfers between devices with their start and end apart: 3, of which 3 were waited for; matrix products, arithmetic and copies ran while one was open for 10% of the time, Pallas kernels for 0%

commit v1 on v0

v1 whole, which is shorter than its diff:
```python
import functools

import jax
import jax.numpy as jnp
from jax import lax
from jax.experimental import pallas as pl
from jax.experimental.pallas import tpu as pltpu
from jax.sharding import PartitionSpec as P

R = 256
TILE = 128
STEPS = 3
ROW_TILES = 8
COL_TILES = 8
SLOTS = 24
WIDE = 2 * TILE


learn_rate = 0.05
weight_decay = 0.02
user_scale = 1.0 / 64.0

CORE_GROUPS = [[0, 2, 4, 6], [1, 3, 5, 7]]


def passed_along(value, axis, steps):
    count = lax.axis_size(axis)
    pairs = [(source, (source + steps) % count) for source in range(count)]
    return lax.ppermute(value, axis, pairs)


def chunk_body(step, part, parts, has_total, split, *refs):
    refs = list(refs)
    ids_ref, count_ref, users_ref, panel_ref, rating_ref = refs[:5]
    refs = refs[5:]
    if has_total:
        total_ref = refs.pop(0)
    if step == STEPS - 1 and part > 0:
        refs.pop(0)
    new_ref = refs.pop(0)
    if split:
        mine_ref, theirs_ref = refs.pop(0), refs.pop(0)
    else:
        out_ref = refs.pop(0)
    slot_ref, residual, rounded = refs[:3]
    if split:
        out_ref = refs[3]
    columns = COL_TILES * TILE // parts

    def clear(index, carry):
        slot_ref[index] = -1
        return carry

    lax.fori_loop(0, ROW_TILES * COL_TILES, clear, 0, unroll=True)
    live_count = count_ref[step, 0]
    for slot in range(SLOTS):
        slot_ref[ids_ref[step, slot]] = jnp.where(slot < live_count, slot, -1)

    rounded[...] = panel_ref[...].astype(jnp.bfloat16)
    contract_last = (((1,), (1,)), ((), ()))
    contract_first = (((0,), (0,)), ((), ()))
    for wide in range(columns // WIDE):
        cols = slice(wide * WIDE, (wide + 1) * WIDE)
        for block in range(ROW_TILES // 2):
            rows = slice(block * WIDE, (block + 1) * WIDE)
            predicted = lax.dot_general(
                users_ref[rows, :], rounded[cols, :], contract_last, preferred_element_type=jnp.float32
            )
            for down in range(2):
                for across in range(2):
                    tile_row = block * 2 + down
                    tile_col = part * (columns // TILE) + wide * 2 + across
                    slot = slot_ref[tile_row * COL_TILES + tile_col]
                    rating = rating_ref[0, jnp.maximum(slot, 0)].astype(jnp.float32)
                    piece = predicted[down * TILE:(down + 1) * TILE, across * TILE:(across + 1) * TILE]
                    piece = jnp.where(slot >= 0, piece - rating, 0.0).astype(jnp.bfloat16)
                    residual[
                        tile_row * TILE:(tile_row + 1) * TILE,
                        wide * WIDE + across * TILE:wide * WIDE + (across + 1) * TILE,
                    ] = piece
        item_grad = lax.dot_general(
            residual[:, cols], users_ref[...], contract_first, preferred_element_type=jnp.float32
        )
        held = panel_ref[cols, :]
        new_ref[cols, :] = held - learn_rate * (item_grad + weight_decay * held)
    for block in range(ROW_TILES // 2):
        rows = slice(block * WIDE, (block + 1) * WIDE)
        user_part = jnp.dot(residual[rows, :], rounded[...], preferred_element_type=jnp.float32)
        if has_total:
            user_part = total_ref[rows, :] + user_part
        out_ref[rows, :] = user_part
    if split:
        core = lax.axis_index("item") % 2
        for index in range(ROW_TILES // 2):
            for ref, own in ((mine_ref, core), (theirs_ref, 1 - core)):
                start = pl.multiple_of((2 * index + own) * TILE, TILE)
                ref[index] = out_ref[pl.ds(start, TILE), :]


def chunk_step(step, part, parts, ids, counts, users, panel, whole_panel, ratings, total, placed):
    columns = COL_TILES * TILE // parts
    split = step == STEPS - 1 and part == parts - 1
    has_total = total is not None
    smem = pl.BlockSpec(memory_space=pltpu.SMEM)

    def whole(shape):
        return pl.BlockSpec(shape, lambda i: (0,) * len(shape))

    where = part if whole_panel else 0
    operands = [ids, counts, users, panel, ratings]
    in_specs = [
        smem,
        smem,
        whole(users.shape),
        pl.BlockSpec((columns, R), lambda i: (where, 0)),
        pl.BlockSpec((1, SLOTS, TILE, TILE), lambda i: (step, 0, 0, 0)),
    ]
    aliases = {}
    rows_shape = (ROW_TILES * TILE, R)
    if has_total:
        if not split:
            aliases[len(operands)] = 1
        operands.append(total)
        in_specs.append(whole(rows_shape))
    if step == STEPS - 1:
        new_shape = jax.ShapeDtypeStruct((COL_TILES * TILE, R), jnp.float32)
        new_spec = pl.BlockSpec((columns, R), lambda i: (part, 0))
        if part > 0:
            aliases[len(operands)] = 0
            operands.append(placed)
            in_specs.append(pl.BlockSpec(memory_space=pl.ANY))
    else:
        new_shape = jax.ShapeDtypeStruct((columns, R), jnp.float32)
        new_spec = whole((columns, R))
    scratch = [
        pltpu.SMEM((ROW_TILES * COL_TILES,), jnp.int32),
        pltpu.VMEM((ROW_TILES * TILE, columns), jnp.bfloat16),
        pltpu.VMEM((columns, R), jnp.bfloat16),
    ]
    if split:
        half = (ROW_TILES // 2, TILE, R)
        out_shape = (new_shape,) + (jax.ShapeDtypeStruct(half, jnp.float32),) * 2
        out_specs = (new_spec, whole(half), whole(half))
        scratch.append(pltpu.VMEM(rows_shape, jnp.float32))
    else:
        out_shape = (new_shape, jax.ShapeDtypeStruct(rows_shape, jnp.float32))
        out_specs = (new_spec, whole(rows_shape))
    flops = 3 * 2 * ROW_TILES * TILE * columns * R
    return pl.pallas_call(
        functools.partial(chunk_body, step, part, parts, has_total, split),
        grid=(1,),
        in_specs=in_specs,
        out_specs=out_specs,
        out_shape=out_shape,
        scratch_shapes=scratch,
        input_output_aliases=aliases,
        cost_estimate=pl.CostEstimate(flops=flops, bytes_accessed=4 << 20, transcendentals=0),
        name="chunk_%d_%d" % (step, part),
    )(*operands)


def shards(user_factors, item_panels, ratings, tile_ids, tile_count):
    parts = 2
    ids = tile_ids.reshape(STEPS, SLOTS)
    counts = tile_count.reshape(STEPS, 1)
    pieces = [item_panels] * parts
    total = None
    placed = None
    for step in range(STEPS):
        moved = []
        for part in range(parts):
            results = chunk_step(
                step, part, parts, ids, counts, user_factors, pieces[part], step == 0, ratings, total, placed
            )
            if step == STEPS - 1:
                placed = results[0]
            else:
                moved.append(passed_along(results[0], "user", 1))
            total = results[1]
        pieces = moved
    mine, theirs = results[1], results[2]
    pairs = [(source, source ^ 1) for source in range(lax.axis_size("item"))]
    joined = mine + lax.ppermute(theirs, "item", pairs)
    spread = lax.all_to_all(joined, "item", 0, 0, axis_index_groups=CORE_GROUPS)
    share_grad = jnp.sum(spread, axis=0) * user_scale
    return (placed, share_grad)


def solution(mesh):
    in_specs = (
        P("user", None),
        P(("user", "item"), None),
        P(None, "user", "item", None),
        P(None, "user", "item"),
        P(None, "user", "item"),
    )
    out_specs = (P(("user", "item"), None), P(("user", "item"), None))
    return jax.shard_map(shards, mesh=mesh, in_specs=in_specs, out_specs=out_specs, check_vma=False)
```

time: 155 us -> 92.2 us (0.59)
  waiting for transfers between devices: 76.2 us -> 31.5 us
  matrix products: 31.8 us -> 0 us
  Pallas kernels: 0 us -> 23.7 us
  between operations: 14.4 us -> 0.69 us
  blocking collectives: 0 us -> 12.4 us
  starting transfers between devices: 6.62 us -> 15.7 us
  local copies, waits for them, and re-layouts: 14.4 us -> 5.78 us
  other arithmetic: 10.4 us -> 1.81 us
    dot_general x15 -> x0, matrix products: 31.8 us -> none  [the longest x3 9.76 us: padded_update(): jnp.einsum('ka,kir->air', row_pick, user_parts, precision=lax.Precision.H...]
    reduce_scatter x1 -> x0, waiting for transfers between devices: 26.8 us -> none  [shards(): lax.psum_scatter(total_grad, 'item', scatter_dimension=0, tiled=True)]
    pallas_call x0 -> x6, Pallas kernels: none -> 23.7 us  [chunk_step(): pl.pallas_call(functools.partial(chunk_body, step, part, parts, has_total...]
    ppermute x2 -> x4, waiting for transfers between devices: 49.3 us -> 29.8 us  [passed_along(): return lax.ppermute(value, axis, pairs)]
    all_to_all x0 -> x1, blocking collectives: none -> 12.4 us  [shards(): spread = lax.all_to_all(joined, 'item', 0, 0, axis_index_groups=CORE_GROUPS)]
    gather x6 -> x0, local copies, waits for them, and re-layouts: 8.68 us -> none  [the longest x3 4.37 us: padded_update(): item_block.astype(jnp.bfloat16).reshape(col_tiles, TILE, R)[col_index]]
    ppermute x2 -> x4, starting transfers between devices: 6.59 us -> 11.7 us  [passed_along(): return lax.ppermute(value, axis, pairs)]
    convert_element_type x6 -> x0, other arithmetic: 4.48 us -> none  [the longest x3 2.61 us: padded_update(): item_block.astype(jnp.bfloat16).reshape(col_tiles, TILE, R)[col_index]]
  transfers between devices with their start and end apart: 3 -> 5, of which waited for: 3 -> 5; matrix products, arithmetic and copies ran while one was open for 10% -> 0% of each run, Pallas kernels for 0% -> 17%
where the time goes in v1:
time: 92.2 us; the launch traced here: 91.7 us
  waiting for transfers between devices  31.5 us (34%)
  Pallas kernels  23.7 us (26%)
  starting transfers between devices  15.7 us (17%)
  blocking collectives  12.4 us (13%)
  local copies, waits for them, and re-layouts  5.78 us (6%)
  other arithmetic  1.81 us (2%)
    ppermute x4, waiting for transfers between devices, passed_along(): return lax.ppermute(value, axis, pairs)  29.8 us
    pallas_call x6, Pallas kernels, chunk_step(): pl.pallas_call(functools.partial(chunk_body, step, part, parts, has_total...  23.7 us
    all_to_all x1, blocking collectives, shards(): spread = lax.all_to_all(joined, 'item', 0, 0, axis_index_groups=CORE_GROUPS)  12.4 us
    ppermute x4, starting transfers between devices, passed_along(): return lax.ppermute(value, axis, pairs)  11.7 us
    unnamed x9, local copies, waits for them, and re-layouts  4.46 us
    ppermute x1, starting transfers between devices, shards(): joined = mine + lax.ppermute(theirs, 'item', pairs)  3.97 us
  transfers between devices with their start and end apart: 5, of which 5 were waited for; matrix products, arithmetic and copies ran while one was open for 0% of the time, Pallas kernels for 17%

profile of v1, /device:TPU:1, one launch (start us, length us, event | category | flops | bytes accessed | tf_op | source)
XLA Modules:
  0.0 91.7 jit_solution(13082638663665388844)
XLA Ops:
  0.6 1.3 %copy.17.refs_1_ = s32[3,1]{1,0:T(4,128)} copy(s32[3,1]{0,1:T(1,128)} %bitcast.10) | data formatting | bytes 24 | tf_op jit(solution)/shard_map/reshape | solution.py:165
  1.9 1.3 %copy.20 = s32[3,24,1]{1,0,2:T(4,128)} copy(s32[3,24,1]{1,2,0:T(1,128)} %param.8) | data formatting | bytes 576
  3.2 3.7 %chunk_0_0.1 = (f32[512,256]{1,0:T(8,128)}, f32[1024,256]{1,0:T(8,128)}) custom-call(s32[3,24]{1,0:T(4,128)} %bitcast.4, s32[3,1]{1,0:T(4,128)} %copy.17.refs_1_, bf16[1024,256]{1,0:T(8,128)(2,1)} %refs_2_.11, f32[1024,256]{1,0:T(8,128)} %refs_3_.3, bf16[3,24,128,128]{3,2,1,0:T(8,128)(2,1)} %refs_4_.11), custom_call_target="tpu_custom_call" | custom-call | flops 805306368 | bytes 4194304 | tf_op jit(solution)/shard_map/chunk_0_0/pallas_call | solution.py:149
  6.9 4.3 %collective-permute-start.1 = (f32[512,256]{1,0:T(8,128)}, f32[512,256]{1,0:T(8,128)S(1)}, u32[]{:S(2)}, u32[]{:S(2)}) collective-permute-start(f32[512,256]{1,0:T(8,128)} %get-tuple-element.17), channel_id=1, source_target_pairs={{0,8},{8,16},{16,24},{24,32},{32,40},{40,48},{48,56},{56,64},{64,7... | collective-permute-start | bytes 1572872 | tf_op jit(solution)/shard_map/ppermute | solution.py:29
  11.2 4.0 %chunk_0_1.1 = (f32[512,256]{1,0:T(8,128)}, f32[1024,256]{1,0:T(8,128)}) custom-call(s32[3,24]{1,0:T(4,128)} %bitcast.5, s32[3,1]{1,0:T(4,128)} %copy.17.refs_1_, bf16[1024,256]{1,0:T(8,128)(2,1)} %refs_2_.11, f32[1024,256]{1,0:T(8,128)} %refs_3_.3, bf16[3,24,128,128]{3,2,1,0:T(8,128)(2,1)} %refs_4_.11, ...), custom_call_target="tpu_custom_call", output_to_operand_aliasing={{1}: (5, {})} | custom-call | flops 805306368 | bytes 4194304 | tf_op jit(solution)/shard_map/chunk_0_1/pallas_call | solution.py:149
  15.2 3.6 %collective-permute-start = (f32[512,256]{1,0:T(8,128)}, f32[512,256]{1,0:T(8,128)S(1)}, u32[]{:S(2)}, u32[]{:S(2)}) collective-permute-start(f32[512,256]{1,0:T(8,128)} %get-tuple-element.16), channel_id=1, source_target_pairs={{0,8},{8,16},{16,24},{24,32},{32,40},{40,48},{48,56},{56,64},{64,7... | collective-permute-start | bytes 1572872 | tf_op jit(solution)/shard_map/ppermute | solution.py:29
  18.8 14.3 %collective-permute-done.1.refs_3_ = f32[512,256]{1,0:T(8,128)S(1)} collective-permute-done((f32[512,256]{1,0:T(8,128)}, f32[512,256]{1,0:T(8,128)S(1)}, u32[]{:S(2)}, u32[]{:S(2)}) %collective-permute-start.1) | collective-permute-done | bytes 524320 | tf_op jit(solution)/shard_map/ppermute | solution.py:29
  33.1 0.0 copy-start.3
  33.1 0.8 copy-done.3
  33.9 4.0 %chunk_1_0.1 = (f32[512,256]{1,0:T(8,128)}, f32[1024,256]{1,0:T(8,128)}) custom-call(s32[3,24]{1,0:T(4,128)} %bitcast.6, s32[3,1]{1,0:T(4,128)} %copy.17.refs_1_, bf16[1024,256]{1,0:T(8,128)(2,1)} %refs_2_.11, f32[512,256]{1,0:T(8,128)} %copy-done.3, bf16[3,24,128,128]{3,2,1,0:T(8,128)(2,1)} %refs_4_.11, ...), custom_call_target="tpu_custom_call", output_to_operand_aliasing={{1}: (5, {})} | custom-call | flops 805306368 | bytes 4194304 | tf_op jit(solution)/shard_map/chunk_1_0/pallas_call | solution.py:149
  37.9 1.9 %collective-permute-start.3 = (f32[512,256]{1,0:T(8,128)}, f32[512,256]{1,0:T(8,128)S(1)}, u32[]{:S(2)}, u32[]{:S(2)}) collective-permute-start(f32[512,256]{1,0:T(8,128)} %get-tuple-element.21), channel_id=1, source_target_pairs={{0,8},{8,16},{16,24},{24,32},{32,40},{40,48},{48,56},{56,64},{64,7... | collective-permute-start | bytes 1572872 | tf_op jit(solution)/shard_map/ppermute | solution.py:29
  39.8 4.5 %collective-permute-done.refs_3_ = f32[512,256]{1,0:T(8,128)S(1)} collective-permute-done((f32[512,256]{1,0:T(8,128)}, f32[512,256]{1,0:T(8,128)S(1)}, u32[]{:S(2)}, u32[]{:S(2)}) %collective-permute-start) | collective-permute-done | bytes 524320 | tf_op jit(solution)/shard_map/ppermute | solution.py:29
  44.3 0.0 copy-start
  44.3 0.8 copy-done
  45.1 4.0 %chunk_1_1.1 = (f32[512,256]{1,0:T(8,128)}, f32[1024,256]{1,0:T(8,128)}) custom-call(s32[3,24]{1,0:T(4,128)} %bitcast.7, s32[3,1]{1,0:T(4,128)} %copy.17.refs_1_, bf16[1024,256]{1,0:T(8,128)(2,1)} %refs_2_.11, f32[512,256]{1,0:T(8,128)} %copy-done, bf16[3,24,128,128]{3,2,1,0:T(8,128)(2,1)} %refs_4_.11, ...), custom_call_target="tpu_custom_call", output_to_operand_aliasing={{1}: (5, {})} | custom-call | flops 805306368 | bytes 4194304 | tf_op jit(solution)/shard_map/chunk_1_1/pallas_call | solution.py:149
  49.1 1.9 %collective-permute-start.2 = (f32[512,256]{1,0:T(8,128)}, f32[512,256]{1,0:T(8,128)S(1)}, u32[]{:S(2)}, u32[]{:S(2)}) collective-permute-start(f32[512,256]{1,0:T(8,128)} %get-tuple-element.20), channel_id=1, source_target_pairs={{0,8},{8,16},{16,24},{24,32},{32,40},{40,48},{48,56},{56,64},{64,7... | collective-permute-start | bytes 1572872 | tf_op jit(solution)/shard_map/ppermute | solution.py:29
  51.0 3.6 %collective-permute-done.3.refs_3_ = f32[512,256]{1,0:T(8,128)S(1)} collective-permute-done((f32[512,256]{1,0:T(8,128)}, f32[512,256]{1,0:T(8,128)S(1)}, u32[]{:S(2)}, u32[]{:S(2)}) %collective-permute-start.3) | collective-permute-done | bytes 524320 | tf_op jit(solution)/shard_map/ppermute | solution.py:29
  54.7 0.0 copy-start.1
  54.7 0.8 copy-done.1
  55.5 4.0 %chunk_2_0.1 = (f32[1024,256]{1,0:T(8,128)}, f32[1024,256]{1,0:T(8,128)}) custom-call(s32[3,24]{1,0:T(4,128)} %bitcast.8, s32[3,1]{1,0:T(4,128)} %copy.17.refs_1_, bf16[1024,256]{1,0:T(8,128)(2,1)} %refs_2_.11, f32[512,256]{1,0:T(8,128)} %copy-done.1, bf16[3,24,128,128]{3,2,1,0:T(8,128)(2,1)} %refs_4_.11, ...), custom_call_target="tpu_custom_call", output_to_operand_aliasing={{1}: (5, {})} | custom-call | flops 805306368 | bytes 4194304 | tf_op jit(solution)/shard_map/chunk_2_0/pallas_call | solution.py:149
  59.5 7.3 %collective-permute-done.2.refs_3_ = f32[512,256]{1,0:T(8,128)S(1)} collective-permute-done((f32[512,256]{1,0:T(8,128)}, f32[512,256]{1,0:T(8,128)S(1)}, u32[]{:S(2)}, u32[]{:S(2)}) %collective-permute-start.2) | collective-permute-done | bytes 524320 | tf_op jit(solution)/shard_map/ppermute | solution.py:29
  66.8 0.0 copy-start.2
  66.8 0.8 copy-done.2
  67.6 4.1 %chunk_2_1.1 = (f32[1024,256]{1,0:T(8,128)}, f32[4,128,256]{2,1,0:T(8,128)}, f32[4,128,256]{2,1,0:T(8,128)}) custom-call(s32[3,24]{1,0:T(4,128)} %bitcast.9, s32[3,1]{1,0:T(4,128)} %copy.17.refs_1_, bf16[1024,256]{1,0:T(8,128)(2,1)} %refs_2_.11, f32[512,256]{1,0:T(8,128)} %copy-done.2, ...), custom_call_target="tpu_custom_call", output_to_operand_aliasing={{0}: (6, {})} | custom-call | flops 805306368 | bytes 4194304 | tf_op jit(solution)/shard_map/chunk_2_1/pallas_call | solution.py:149
  71.7 4.0 %collective-permute-start.4 = (f32[4,128,256]{2,1,0:T(8,128)}, f32[4,128,256]{2,1,0:T(8,128)S(1)}, u32[]{:S(2)}, u32[]{:S(2)}) collective-permute-start(f32[4,128,256]{2,1,0:T(8,128)} %get-tuple-element.27), channel_id=1, source_target_pairs={{0,1},{1,0},{2,3},{3,2},{4,5},{5,4},{6,7},{7,6},{8,9},{9,8},{10,11... | collective-permute-start | bytes 1572872 | tf_op jit(solution)/shard_map/ppermute | solution.py:183
  75.7 1.7 %collective-permute-done.4 = f32[4,128,256]{2,1,0:T(8,128)S(1)} collective-permute-done((f32[4,128,256]{2,1,0:T(8,128)}, f32[4,128,256]{2,1,0:T(8,128)S(1)}, u32[]{:S(2)}, u32[]{:S(2)}) %collective-permute-start.4) | collective-permute-done | bytes 524320 | tf_op jit(solution)/shard_map/ppermute | solution.py:183
  77.4 1.1 %add.3 = f32[4,128,256]{2,1,0:T(8,128)S(1)} add(f32[4,128,256]{2,1,0:T(8,128)} %get-tuple-element.26, f32[4,128,256]{2,1,0:T(8,128)S(1)} %collective-permute-done.4) | non-fusion elementwise | flops 131072 | bytes 1572864 | tf_op jit(solution)/shard_map/add | solution.py:183
  78.5 12.4 %all_to_all.5 = f32[4,128,256]{2,1,0:T(8,128)S(1)} all-to-all(f32[4,128,256]{2,1,0:T(8,128)S(1)} %add.3), channel_id=1, replica_groups={{0,2,4,6},{1,3,5,7},{8,10,12,14},{9,11,13,15},{16,18,20,22},{17,19,21,2..., dimensions={0} | all-to-all | bytes 1048576 | tf_op jit(solution)/shard_map/all_to_all | solution.py:184
  91.0 0.7 broadcast_multiply_fusion
  (1 shorter events, 0.0 us)
Async XLA Ops:
  6.9 26.2 %collective-permute-start.1 = (f32[512,256]{1,0:T(8,128)}, f32[512,256]{1,0:T(8,128)S(1)}, u32[]{:S(2)}, u32[]{:S(2)}) collective-permute-start(f32[512,256]{1,0:T(8,128)} %get-tuple-element.17), channel_id=1, source_target_pairs={{0,8},{8,16},{16,24},{24,32},{32,40},{40,48},{48,56},{56,64},{64,7... | collective-permute-start | bytes 1572872 | tf_op jit(solution)/shard_map/ppermute | solution.py:29
  15.2 29.1 %collective-permute-start = (f32[512,256]{1,0:T(8,128)}, f32[512,256]{1,0:T(8,128)S(1)}, u32[]{:S(2)}, u32[]{:S(2)}) collective-permute-start(f32[512,256]{1,0:T(8,128)} %get-tuple-element.16), channel_id=1, source_target_pairs={{0,8},{8,16},{16,24},{24,32},{32,40},{40,48},{48,56},{56,64},{64,7... | collective-permute-start | bytes 1572872 | tf_op jit(solution)/shard_map/ppermute | solution.py:29
  33.1 0.8 copy-start.3
  37.9 16.8 %collective-permute-start.3 = (f32[512,256]{1,0:T(8,128)}, f32[512,256]{1,0:T(8,128)S(1)}, u32[]{:S(2)}, u32[]{:S(2)}) collective-permute-start(f32[512,256]{1,0:T(8,128)} %get-tuple-element.21), channel_id=1, source_target_pairs={{0,8},{8,16},{16,24},{24,32},{32,40},{40,48},{48,56},{56,64},{64,7... | collective-permute-start | bytes 1572872 | tf_op jit(solution)/shard_map/ppermute | solution.py:29
  44.3 0.8 copy-start
  49.1 17.7 %collective-permute-start.2 = (f32[512,256]{1,0:T(8,128)}, f32[512,256]{1,0:T(8,128)S(1)}, u32[]{:S(2)}, u32[]{:S(2)}) collective-permute-start(f32[512,256]{1,0:T(8,128)} %get-tuple-element.20), channel_id=1, source_target_pairs={{0,8},{8,16},{16,24},{24,32},{32,40},{40,48},{48,56},{56,64},{64,7... | collective-permute-start | bytes 1572872 | tf_op jit(solution)/shard_map/ppermute | solution.py:29
  54.7 0.8 copy-start.1
  66.8 0.8 copy-start.2
  71.7 5.7 %collective-permute-start.4 = (f32[4,128,256]{2,1,0:T(8,128)}, f32[4,128,256]{2,1,0:T(8,128)S(1)}, u32[]{:S(2)}, u32[]{:S(2)}) collective-permute-start(f32[4,128,256]{2,1,0:T(8,128)} %get-tuple-element.27), channel_id=1, source_target_pairs={{0,1},{1,0},{2,3},{3,2},{4,5},{5,4},{6,7},{7,6},{8,9},{9,8},{10,11... | collective-permute-start | bytes 1572872 | tf_op jit(solution)/shard_map/ppermute | solution.py:183

commit v2 on v0

v2 whole, which is shorter than its diff:
```python
import functools

import jax
import jax.numpy as jnp
from jax import lax
from jax.experimental import pallas as pl
from jax.experimental.pallas import tpu as pltpu
from jax.sharding import PartitionSpec as P

R = 256
TILE = 128
STEPS = 3
ROW_TILES = 8
COL_TILES = 8
SLOTS = 24
ROWS = ROW_TILES * TILE
COLS = COL_TILES * TILE
WIDE = 2 * TILE
HALF = COLS // 2


learn_rate = 0.05
weight_decay = 0.02
user_scale = 1.0 / 64.0

CORE_GROUPS = [[0, 2, 4, 6], [1, 3, 5, 7]]

smem = pl.BlockSpec(memory_space=pltpu.SMEM)
vmem = pl.BlockSpec(memory_space=pltpu.VMEM)
anywhere = pl.BlockSpec(memory_space=pl.ANY)
contract_last = (((1,), (1,)), ((), ()))
contract_first = (((0,), (0,)), ((), ()))


def passed_along(value, axis, steps):
    count = lax.axis_size(axis)
    pairs = [(source, (source + steps) % count) for source in range(count)]
    return lax.ppermute(value, axis, pairs)


def find_slots(step, first_col, ids_ref, count_ref, slot_ref):
    for tile in range(ROW_TILES * COL_TILES):
        slot_ref[tile] = -1
    live_count = count_ref[0, 0, step]
    for slot in range(SLOTS):
        slot_ref[ids_ref[step, 0, slot]] = jnp.where(slot < live_count, slot, -1)


def fill_residual(first_col, users_ref, rounded_ref, rating_at, slot_ref, residual_ref, before_ratings=None):
    for wide in range(HALF // WIDE):
        cols = slice(wide * WIDE, (wide + 1) * WIDE)
        for block in range(ROWS // WIDE):
            rows = slice(block * WIDE, (block + 1) * WIDE)
            predicted = lax.dot_general(
                users_ref[rows, :], rounded_ref[cols, :], contract_last, preferred_element_type=jnp.float32
            )
            if before_ratings is not None:
                before_ratings()
                before_ratings = None
            for down in range(2):
                for across in range(2):
                    tile_row = block * 2 + down
                    tile_col = first_col + wide * 2 + across
                    slot = slot_ref[tile_row * COL_TILES + tile_col]
                    rating = rating_at(jnp.maximum(slot, 0)).astype(jnp.float32)
                    piece = predicted[down * TILE:(down + 1) * TILE, across * TILE:(across + 1) * TILE]
                    piece = jnp.where(slot >= 0, piece - rating, 0.0).astype(jnp.bfloat16)
                    residual_ref[
                        tile_row * TILE:(tile_row + 1) * TILE,
                        wide * WIDE + across * TILE:wide * WIDE + (across + 1) * TILE,
                    ] = piece


def update_panel(users_ref, panel_ref, residual_ref, new_ref):
    for wide in range(HALF // WIDE):
        cols = slice(wide * WIDE, (wide + 1) * WIDE)
        item_grad = lax.dot_general(
            residual_ref[:, cols], users_ref[...], contract_first, preferred_element_type=jnp.float32
        )
        held = panel_ref[cols, :]
        new_ref[cols, :] = held - learn_rate * (item_grad + weight_decay * held)


def first_kernel(ids_ref, count_ref, users_hbm, panel_hbm, rating_hbm, new_ref, residual_ref, rounded_ref,
                 slot_ref, users_ref, panel_ref, rating_ref, users_sem, panel_sem, rating_sem):
    panel_copy = pltpu.make_async_copy(panel_hbm.at[pl.ds(0, HALF)], panel_ref, panel_sem)
    users_copy = pltpu.make_async_copy(users_hbm, users_ref, users_sem)
    rating_copy = pltpu.make_async_copy(rating_hbm.at[0], rating_ref, rating_sem)
    panel_copy.start()
    users_copy.start()
    rating_copy.start()
    find_slots(0, 0, ids_ref, count_ref, slot_ref)
    panel_copy.wait()
    rounded_ref[...] = panel_ref[...].astype(jnp.bfloat16)
    users_copy.wait()
    fill_residual(0, users_ref, rounded_ref, lambda slot: rating_ref[slot], slot_ref, residual_ref, rating_copy.wait)
    update_panel(users_ref, panel_ref, residual_ref, new_ref)


def add_user_part(blocks, total_ref, out_ref):
    for block in range(ROWS // WIDE):
        rows = slice(block * WIDE, (block + 1) * WIDE)
        part = None
        for residual_ref, rounded_ref in blocks:
            term = jnp.dot(residual_ref[rows, :], rounded_ref[...], preferred_element_type=jnp.float32)
            part = term if part is None else part + term
        if total_ref is not None:
            part = part + total_ref[rows, :]
        out_ref[rows, :] = part


def early_kernel(step, ids_ref, count_ref, users_ref, panel_ref, rating_ref, new_ref, residual_ref, rounded_ref,
                 slot_ref):
    find_slots(step, 0, ids_ref, count_ref, slot_ref)
    rounded_ref[...] = panel_ref[...].astype(jnp.bfloat16)
    fill_residual(0, users_ref, rounded_ref, lambda slot: rating_ref[step, slot], slot_ref, residual_ref)
    update_panel(users_ref, panel_ref, residual_ref, new_ref)


def late_kernel(step, *refs):
    refs = list(refs)
    ids_ref, count_ref, users_ref, panel_ref, rating_ref, early_residual, early_rounded = refs[:7]
    total_ref = refs.pop(7) if step > 0 else None
    new_ref, out_ref, slot_ref, residual_ref, rounded_ref = refs[7:]
    if step == 0:
        panel_ref = panel_ref.at[pl.ds(HALF, HALF)]
    find_slots(step, COL_TILES // 2, ids_ref, count_ref, slot_ref)
    rounded_ref[...] = panel_ref[...].astype(jnp.bfloat16)
    fill_residual(
        COL_TILES // 2, users_ref, rounded_ref, lambda slot: rating_ref[step, slot], slot_ref, residual_ref
    )
    update_panel(users_ref, panel_ref, residual_ref, new_ref)
    add_user_part([(early_residual, early_rounded), (residual_ref, rounded_ref)], total_ref, out_ref)


def last_early_kernel(step, ids_ref, count_ref, users_ref, panel_ref, rating_ref, total_ref, new_ref, out_ref,
                      slot_ref, residual_ref, rounded_ref):
    find_slots(step, 0, ids_ref, count_ref, slot_ref)
    rounded_ref[...] = panel_ref[...].astype(jnp.bfloat16)
    fill_residual(0, users_ref, rounded_ref, lambda slot: rating_ref[step, slot], slot_ref, residual_ref)
    update_panel(users_ref, panel_ref, residual_ref, new_ref)
    add_user_part([(residual_ref, rounded_ref)], total_ref, out_ref)


def last_late_kernel(step, ids_ref, count_ref, users_ref, panel_ref, rating_ref, total_ref,
                     residual_ref, mine_ref, theirs_ref, slot_ref, rounded_ref):
    find_slots(step, COL_TILES // 2, ids_ref, count_ref, slot_ref)
    rounded_ref[...] = panel_ref[...].astype(jnp.bfloat16)
    fill_residual(
        COL_TILES // 2, users_ref, rounded_ref, lambda slot: rating_ref[step, slot], slot_ref, residual_ref
    )
    core = lax.axis_index("item") % 2
    for index in range(ROW_TILES // 2):
        for ref, own in ((theirs_ref, 1 - core), (mine_ref, core)):
            rows = pl.ds(pl.multiple_of((2 * index + own) * TILE, TILE), TILE)
            part = jnp.dot(residual_ref[rows, :], rounded_ref[...], preferred_element_type=jnp.float32)
            ref[index] = (part + total_ref[rows, :]) * user_scale


def last_update_kernel(users_ref, panel_ref, residual_ref, placed_ref, new_ref):
    new_ref[:HALF, :] = placed_ref[...]
    update_panel(users_ref, panel_ref, residual_ref, new_ref.at[pl.ds(HALF, HALF)])


panel_half = jax.ShapeDtypeStruct((HALF, R), jnp.float32)
residual_half = jax.ShapeDtypeStruct((ROWS, HALF), jnp.bfloat16)
rounded_half = jax.ShapeDtypeStruct((HALF, R), jnp.bfloat16)
row_sum = jax.ShapeDtypeStruct((ROWS, R), jnp.float32)
quarter_sums = jax.ShapeDtypeStruct((ROW_TILES // 2, TILE, R), jnp.float32)
slot_scratch = pltpu.SMEM((ROW_TILES * COL_TILES,), jnp.int32)
half_scratch = [slot_scratch, pltpu.VMEM((ROWS, HALF), jnp.bfloat16), pltpu.VMEM((HALF, R), jnp.bfloat16)]


def kernel_call(body, name, matmuls, operands, in_specs, out_shape, scratch, aliases=None):
    return pl.pallas_call(
        body,
        in_specs=in_specs,
        out_specs=jax.tree.map(lambda _: vmem, out_shape),
        out_shape=out_shape,
        scratch_shapes=scratch,
        input_output_aliases=aliases or {},
        compiler_params=pltpu.CompilerParams(vmem_limit_bytes=16 << 20),
        cost_estimate=pl.CostEstimate(
            flops=matmuls * 2 * ROWS * HALF * R, bytes_accessed=3 << 20, transcendentals=0
        ),
        name=name,
    )(*operands)


def shards(user_factors, item_panels, ratings, tile_ids, tile_count):
    ids = tile_ids.transpose(0, 2, 1)
    counts = tile_count.transpose(1, 2, 0)
    lists = [pltpu.with_memory_space_constraint(a, pltpu.HBM) for a in (ids, counts)]
    list_specs = [smem, smem]

    new, early_residual, early_rounded = kernel_call(
        first_kernel, "first", 2,
        lists + [pltpu.with_memory_space_constraint(a, pltpu.HBM) for a in (user_factors, item_panels, ratings)],
        list_specs + [anywhere] * 3,
        (panel_half, residual_half, rounded_half),
        [
            slot_scratch,
            pltpu.VMEM((ROWS, R), jnp.bfloat16),
            pltpu.VMEM((HALF, R), jnp.float32),
            pltpu.VMEM((SLOTS, TILE, TILE), jnp.bfloat16),
            pltpu.SemaphoreType.DMA,
            pltpu.SemaphoreType.DMA,
            pltpu.SemaphoreType.DMA,
        ],
    )
    new, user_factors, late_panel, ratings = lax.optimization_barrier((new, user_factors, item_panels, ratings))
    early = passed_along(new, "user", 1)
    total = None
    for step in range(STEPS - 1):
        operands = lists + [user_factors, late_panel, ratings, early_residual, early_rounded]
        aliases = {}
        if step > 0:
            aliases = {len(operands): 1}
            operands.append(total)
        new, total = kernel_call(
            functools.partial(late_kernel, step), "late_%d" % step, 4,
            operands, list_specs + [vmem] * (len(operands) - 2), (panel_half, row_sum), half_scratch, aliases,
        )
        late = passed_along(new, "user", 1)
        step += 1
        if step < STEPS - 1:
            new, early_residual, early_rounded = kernel_call(
                functools.partial(early_kernel, step), "early_%d" % step, 2,
                lists + [user_factors, early, ratings], list_specs + [vmem] * 3,
                (panel_half, residual_half, rounded_half), [slot_scratch],
            )
            early = passed_along(new, "user", 1)
        else:
            placed, total = kernel_call(
                functools.partial(last_early_kernel, step), "early_%d" % step, 3,
                lists + [user_factors, early, ratings, total], list_specs + [vmem] * 4,
                (panel_half, row_sum), half_scratch, {5: 1},
            )
        late_panel = late
    residual, mine, theirs = kernel_call(
        functools.partial(last_late_kernel, STEPS - 1), "late_%d" % (STEPS - 1), 2,
        lists + [user_factors, late_panel, ratings, total], list_specs + [vmem] * 4,
        (residual_half, quarter_sums, quarter_sums), [slot_scratch, pltpu.VMEM((HALF, R), jnp.bfloat16)],
    )
    pairs = [(source, source ^ 1) for source in range(lax.axis_size("item"))]
    received = lax.ppermute(theirs, "item", pairs)
    panels = kernel_call(
        last_update_kernel, "last_update", 1,
        [user_factors, late_panel, residual, placed], [vmem] * 4,
        jax.ShapeDtypeStruct((COLS, R), jnp.float32), [],
    )
    spread = lax.all_to_all(mine + received, "item", 0, 0, axis_index_groups=CORE_GROUPS)
    return (panels, jnp.sum(spread, axis=0))


def solution(mesh):
    in_specs = (
        P("user", None),
        P(("user", "item"), None),
        P(None, "user", "item", None),
        P(None, "user", "item"),
        P(None, "user", "item"),
    )
    out_specs = (P(("user", "item"), None), P(("user", "item"), None))
    return jax.shard_map(shards, mesh=mesh, in_specs=in_specs, out_specs=out_specs, check_vma=False)
```

time: 155 us -> 85.1 us (0.55)
  matrix products: 31.8 us -> 0 us
  waiting for transfers between devices: 76.2 us -> 49.1 us
  local copies, waits for them, and re-layouts: 14.4 us -> 0.01 us
  Pallas kernels: 0 us -> 14.3 us
  between operations: 14.4 us -> 0.77 us
  starting transfers between devices: 6.62 us -> 18.9 us
  other arithmetic: 10.4 us -> 1.55 us
    dot_general x15 -> x0, matrix products: 31.8 us -> none  [the longest x3 9.76 us: padded_update(): jnp.einsum('ka,kir->air', row_pick, user_parts, precision=lax.Precision.H...]
    reduce_scatter x1 -> x0, waiting for transfers between devices: 26.8 us -> none  [shards(): lax.psum_scatter(total_grad, 'item', scatter_dimension=0, tiled=True)]
    pallas_call x0 -> x7, Pallas kernels: none -> 14.3 us  [kernel_call(): pl.pallas_call(body, in_specs=in_specs, out_specs=jax.tree.map(lambda _:...]
    ppermute x2 -> x4, waiting for transfers between devices: 49.3 us -> 40.1 us  [passed_along(): return lax.ppermute(value, axis, pairs)]
    gather x6 -> x0, local copies, waits for them, and re-layouts: 8.68 us -> none  [the longest x3 4.37 us: padded_update(): item_block.astype(jnp.bfloat16).reshape(col_tiles, TILE, R)[col_index]]
    all_to_all x0 -> x1, waiting for transfers between devices: none -> 7.43 us  [shards(): lax.all_to_all(mine + received, 'item', 0, 0, axis_index_groups=CORE_GROUPS)]
    ppermute x2 -> x4, starting transfers between devices: 6.59 us -> 11.8 us  [passed_along(): return lax.ppermute(value, axis, pairs)]
    convert_element_type x6 -> x0, other arithmetic: 4.48 us -> none  [the longest x3 2.61 us: padded_update(): item_block.astype(jnp.bfloat16).reshape(col_tiles, TILE, R)[col_index]]
  transfers between devices with their start and end apart: 3 -> 6, of which waited for: 3 -> 6; matrix products, arithmetic and copies ran while one was open for 10% -> 0% of each run, Pallas kernels for 0% -> 11%
where the time goes in v2:
time: 85.1 us; the launch traced here: 84.7 us
  waiting for transfers between devices  49.1 us (58%)
  starting transfers between devices  18.9 us (22%)
  Pallas kernels  14.3 us (17%)
  other arithmetic  1.55 us (2%)
    ppermute x4, waiting for transfers between devices, passed_along(): return lax.ppermute(value, axis, pairs)  40.1 us
    pallas_call x7, Pallas kernels, kernel_call(): pl.pallas_call(body, in_specs=in_specs, out_specs=jax.tree.map(lambda _:...  14.3 us
    ppermute x4, starting transfers between devices, passed_along(): return lax.ppermute(value, axis, pairs)  11.8 us
    all_to_all x1, waiting for transfers between devices, shards(): lax.all_to_all(mine + received, 'item', 0, 0, axis_index_groups=CORE_GROUPS)  7.43 us
    all_to_all x1, starting transfers between devices, shards(): lax.all_to_all(mine + received, 'item', 0, 0, axis_index_groups=CORE_GROUPS)  4.01 us
    ppermute x1, starting transfers between devices, shards(): received = lax.ppermute(theirs, 'item', pairs)  3.16 us
  transfers between devices with their start and end apart: 6, of which 6 were waited for; matrix products, arithmetic and copies ran while one was open for 0% of the time, Pallas kernels for 11%

profile of v2, /device:TPU:1, one launch (start us, length us, event | category | flops | bytes accessed | tf_op | source)
XLA Modules:
  0.0 84.7 jit_solution(11109801751044876476)
XLA Ops:
  0.6 0.0 copy-start
  0.6 0.0 copy-start.2
  0.7 0.0 copy-start.1
  0.7 3.4 %first.1 = (f32[512,256]{1,0:T(8,128)S(1)}, bf16[1024,512]{1,0:T(8,128)(2,1)S(1)}, bf16[512,256]{1,0:T(8,128)(2,1)S(1)}) custom-call(s32[3,1,24]{2,1,0:T(1,128)} %bitcast.2, s32[1,1,3]{2,1,0:T(1,128)} %bitcast.8, bf16[1024,256]{1,0:T(8,128)(2,1)} %users_ref.3, f32[1024,256]{1,0:T(8,128)} %refs_3_, bf16[3,24,128,128]{3,2,1,0:T(8,128)(2,1)} %rating_ref.2), custom_call_target="tpu_custom_call" | custom-call | flops 536870912 | bytes 3145728 | tf_op jit(solution)/shard_map/first/pallas_call | solution.py:175
  4.1 4.4 %collective-permute-start.1 = (f32[512,256]{1,0:T(8,128)S(1)}, f32[512,256]{1,0:T(8,128)S(1)}, u32[]{:S(2)}, u32[]{:S(2)}) collective-permute-start(f32[512,256]{1,0:T(8,128)S(1)} %get-tuple-element.28), channel_id=1, source_target_pairs={{0,8},{8,16},{16,24},{24,32},{32,40},{40,48},{48,56},{56,64},{64,7... | collective-permute-start | bytes 1572872 | tf_op jit(solution)/shard_map/ppermute | solution.py:38
  8.5 0.0 copy-done
  8.5 0.0 copy-done.2
  8.5 0.0 copy-done.1
  8.5 2.1 %late_0.1 = (f32[512,256]{1,0:T(8,128)S(1)}, f32[1024,256]{1,0:T(8,128)S(1)}) custom-call(s32[3,1,24]{2,1,0:T(1,128)} %bitcast.3, s32[1,1,3]{2,1,0:T(1,128)} %bitcast.9, bf16[1024,256]{1,0:T(8,128)(2,1)S(1)} %copy-done.1, f32[1024,256]{1,0:T(8,128)S(1)} %copy-done.2, bf16[3,24,128,128]{3,2,1,0:T(8,128)(2,1)S(1)} %copy-done, ...), custom_call_target="tpu_custom_call" | custom-call | flops 1073741824 | bytes 3145728 | tf_op jit(solution)/shard_map/late_0/pallas_call | solution.py:175
  10.6 3.5 %collective-permute-start = (f32[512,256]{1,0:T(8,128)S(1)}, f32[512,256]{1,0:T(8,128)S(1)}, u32[]{:S(2)}, u32[]{:S(2)}) collective-permute-start(f32[512,256]{1,0:T(8,128)S(1)} %get-tuple-element.27), channel_id=1, source_target_pairs={{0,8},{8,16},{16,24},{24,32},{32,40},{40,48},{48,56},{56,64},{64,7... | collective-permute-start | bytes 1572872 | tf_op jit(solution)/shard_map/ppermute | solution.py:38
  14.2 15.9 %collective-permute-done.1.panel_ref = f32[512,256]{1,0:T(8,128)S(1)} collective-permute-done((f32[512,256]{1,0:T(8,128)S(1)}, f32[512,256]{1,0:T(8,128)S(1)}, u32[]{:S(2)}, u32[]{:S(2)}) %collective-permute-start.1) | collective-permute-done | bytes 524320 | tf_op jit(solution)/shard_map/ppermute | solution.py:38
  30.1 1.6 %early_1.1 = (f32[512,256]{1,0:T(8,128)S(1)}, bf16[1024,512]{1,0:T(8,128)(2,1)S(1)}, bf16[512,256]{1,0:T(8,128)(2,1)S(1)}) custom-call(s32[3,1,24]{2,1,0:T(1,128)} %bitcast.4, s32[1,1,3]{2,1,0:T(1,128)} %bitcast.10, bf16[1024,256]{1,0:T(8,128)(2,1)S(1)} %copy-done.1, f32[512,256]{1,0:T(8,128)S(1)} %collective-permute-done.1.panel_ref, ...), custom_call_target="tpu_custom_call" | custom-call | flops 536870912 | bytes 3145728 | tf_op jit(solution)/shard_map/early_1/pallas_call | solution.py:175
  31.7 1.9 %collective-permute-start.3 = (f32[512,256]{1,0:T(8,128)S(1)}, f32[512,256]{1,0:T(8,128)S(1)}, u32[]{:S(2)}, u32[]{:S(2)}) collective-permute-start(f32[512,256]{1,0:T(8,128)S(1)} %get-tuple-element.33), channel_id=1, source_target_pairs={{0,8},{8,16},{16,24},{24,32},{32,40},{40,48},{48,56},{56,64},{64,7... | collective-permute-start | bytes 1572872 | tf_op jit(solution)/shard_map/ppermute | solution.py:38
  33.6 7.7 %collective-permute-done.refs_3_ = f32[512,256]{1,0:T(8,128)S(1)} collective-permute-done((f32[512,256]{1,0:T(8,128)S(1)}, f32[512,256]{1,0:T(8,128)S(1)}, u32[]{:S(2)}, u32[]{:S(2)}) %collective-permute-start) | collective-permute-done | bytes 524320 | tf_op jit(solution)/shard_map/ppermute | solution.py:38
  41.4 2.1 %late_1.1 = (f32[512,256]{1,0:T(8,128)S(1)}, f32[1024,256]{1,0:T(8,128)S(1)}) custom-call(s32[3,1,24]{2,1,0:T(1,128)} %bitcast.5, s32[1,1,3]{2,1,0:T(1,128)} %bitcast.11, bf16[1024,256]{1,0:T(8,128)(2,1)S(1)} %copy-done.1, f32[512,256]{1,0:T(8,128)S(1)} %collective-permute-done.refs_3_, ...), custom_call_target="tpu_custom_call", output_to_operand_aliasing={{1}: (7, {})} | custom-call | flops 1073741824 | bytes 3145728 | tf_op jit(solution)/shard_map/late_1/pallas_call | solution.py:175
  43.5 1.9 %collective-permute-start.2 = (f32[512,256]{1,0:T(8,128)S(1)}, f32[512,256]{1,0:T(8,128)S(1)}, u32[]{:S(2)}, u32[]{:S(2)}) collective-permute-start(f32[512,256]{1,0:T(8,128)S(1)} %get-tuple-element.32), channel_id=1, source_target_pairs={{0,8},{8,16},{16,24},{24,32},{32,40},{40,48},{48,56},{56,64},{64,7... | collective-permute-start | bytes 1572872 | tf_op jit(solution)/shard_map/ppermute | solution.py:38
  45.4 7.1 %collective-permute-done.3.panel_ref = f32[512,256]{1,0:T(8,128)S(1)} collective-permute-done((f32[512,256]{1,0:T(8,128)S(1)}, f32[512,256]{1,0:T(8,128)S(1)}, u32[]{:S(2)}, u32[]{:S(2)}) %collective-permute-start.3) | collective-permute-done | bytes 524320 | tf_op jit(solution)/shard_map/ppermute | solution.py:38
  52.6 1.9 %early_2.1 = (f32[512,256]{1,0:T(8,128)S(1)}, f32[1024,256]{1,0:T(8,128)S(1)}) custom-call(s32[3,1,24]{2,1,0:T(1,128)} %bitcast.6, s32[1,1,3]{2,1,0:T(1,128)} %bitcast.12, bf16[1024,256]{1,0:T(8,128)(2,1)S(1)} %copy-done.1, f32[512,256]{1,0:T(8,128)S(1)} %collective-permute-done.3.panel_ref, ...), custom_call_target="tpu_custom_call", output_to_operand_aliasing={{1}: (5, {})} | custom-call | flops 805306368 | bytes 3145728 | tf_op jit(solution)/shard_map/early_2/pallas_call | solution.py:175
  54.5 9.3 %collective-permute-done.2.panel_ref = f32[512,256]{1,0:T(8,128)S(1)} collective-permute-done((f32[512,256]{1,0:T(8,128)S(1)}, f32[512,256]{1,0:T(8,128)S(1)}, u32[]{:S(2)}, u32[]{:S(2)}) %collective-permute-start.2) | collective-permute-done | bytes 524320 | tf_op jit(solution)/shard_map/ppermute | solution.py:38
  63.8 1.7 %late_2.1 = (bf16[1024,512]{1,0:T(8,128)(2,1)S(1)}, f32[4,128,256]{2,1,0:T(8,128)S(1)}, f32[4,128,256]{2,1,0:T(8,128)S(1)}) custom-call(s32[3,1,24]{2,1,0:T(1,128)} %bitcast.7, s32[1,1,3]{2,1,0:T(1,128)} %bitcast.13, bf16[1024,256]{1,0:T(8,128)(2,1)S(1)} %copy-done.1, f32[512,256]{1,0:T(8,128)S(1)} %collective-permute-done.2.panel_ref, ...), custom_call_target="tpu_custom_call" | custom-call | flops 536870912 | bytes 3145728 | tf_op jit(solution)/shard_map/late_2/pallas_call | solution.py:175
  65.5 3.2 %collective-permute-start.4 = (f32[4,128,256]{2,1,0:T(8,128)S(1)}, f32[4,128,256]{2,1,0:T(8,128)S(1)}, u32[]{:S(2)}, u32[]{:S(2)}) collective-permute-start(f32[4,128,256]{2,1,0:T(8,128)S(1)} %get-tuple-element.39), channel_id=1, source_target_pairs={{0,1},{1,0},{2,3},{3,2},{4,5},{5,4},{6,7},{7,6},{8,9},{9,8},{10,11... | collective-permute-start | bytes 1572872 | tf_op jit(solution)/shard_map/ppermute | solution.py:246
  68.7 1.5 %collective-permute-done.4 = f32[4,128,256]{2,1,0:T(8,128)S(1)} collective-permute-done((f32[4,128,256]{2,1,0:T(8,128)S(1)}, f32[4,128,256]{2,1,0:T(8,128)S(1)}, u32[]{:S(2)}, u32[]{:S(2)}) %collective-permute-start.4) | collective-permute-done | bytes 524320 | tf_op jit(solution)/shard_map/ppermute | solution.py:246
  70.2 0.9 %add.3 = f32[4,128,256]{2,1,0:T(8,128)} add(f32[4,128,256]{2,1,0:T(8,128)S(1)} %get-tuple-element.38, f32[4,128,256]{2,1,0:T(8,128)S(1)} %collective-permute-done.4) | non-fusion elementwise | flops 131072 | bytes 1572864 | tf_op jit(solution)/shard_map/add | solution.py:252
  71.0 4.0 %all-to-all-start = ((f32[4,128,256]{2,1,0:T(8,128)}), f32[4,128,256]{2,1,0:T(8,128)S(1)}, u32[]{:S(2)}, u32[]{:S(2)}) async-start(f32[4,128,256]{2,1,0:T(8,128)} %add.3), calls=%async_computation | async-start | bytes 1048576 | tf_op jit(solution)/shard_map/all_to_all | solution.py:252
  75.1 1.5 %last_update.1 = f32[1024,256]{1,0:T(8,128)} custom-call(bf16[1024,256]{1,0:T(8,128)(2,1)S(1)} %copy-done.1, f32[512,256]{1,0:T(8,128)S(1)} %collective-permute-done.2.panel_ref, bf16[1024,512]{1,0:T(8,128)(2,1)S(1)} %get-tuple-element.36.residual_ref, f32[512,256]{1,0:T(8,128)S(1)} %get-tuple-element.37.placed_ref), custom_call_target="tpu_custom_call" | custom-call | flops 268435456 | bytes 3145728 | tf_op jit(solution)/shard_map/last_update/pallas_call | solution.py:175
  76.5 7.4 %all-to-all-done = f32[4,128,256]{2,1,0:T(8,128)S(1)} async-done(((f32[4,128,256]{2,1,0:T(8,128)}), f32[4,128,256]{2,1,0:T(8,128)S(1)}, u32[]{:S(2)}, u32[]{:S(2)}) %all-to-all-start) | async-done | bytes 524320 | tf_op jit(solution)/shard_map/all_to_all | solution.py:252
  84.0 0.7 reduce_sum.9
Async XLA Ops:
  0.6 7.9 %copy-start = (bf16[3,24,128,128]{3,2,1,0:T(8,128)(2,1)S(1)}, bf16[3,24,128,128]{3,2,1,0:T(8,128)(2,1)}, u32[]{:S(2)}) copy-start(bf16[3,24,128,128]{3,2,1,0:T(8,128)(2,1)} %rating_ref.2) | copy-start | bytes 7077892
  0.6 7.9 %copy-start.2 = (f32[1024,256]{1,0:T(8,128)S(1)}, f32[1024,256]{1,0:T(8,128)}, u32[]{:S(2)}) copy-start(f32[1024,256]{1,0:T(8,128)} %refs_3_) | copy-start | bytes 3145732
  0.7 7.9 %copy-start.1 = (bf16[1024,256]{1,0:T(8,128)(2,1)S(1)}, bf16[1024,256]{1,0:T(8,128)(2,1)}, u32[]{:S(2)}) copy-start(bf16[1024,256]{1,0:T(8,128)(2,1)} %users_ref.3) | copy-start | bytes 1572868
  4.1 26.0 %collective-permute-start.1 = (f32[512,256]{1,0:T(8,128)S(1)}, f32[512,256]{1,0:T(8,128)S(1)}, u32[]{:S(2)}, u32[]{:S(2)}) collective-permute-start(f32[512,256]{1,0:T(8,128)S(1)} %get-tuple-element.28), channel_id=1, source_target_pairs={{0,8},{8,16},{16,24},{24,32},{32,40},{40,48},{48,56},{56,64},{64,7... | collective-permute-start | bytes 1572872 | tf_op jit(solution)/shard_map/ppermute | solution.py:38
  10.6 30.7 %collective-permute-start = (f32[512,256]{1,0:T(8,128)S(1)}, f32[512,256]{1,0:T(8,128)S(1)}, u32[]{:S(2)}, u32[]{:S(2)}) collective-permute-start(f32[512,256]{1,0:T(8,128)S(1)} %get-tuple-element.27), channel_id=1, source_target_pairs={{0,8},{8,16},{16,24},{24,32},{32,40},{40,48},{48,56},{56,64},{64,7... | collective-permute-start | bytes 1572872 | tf_op jit(solution)/shard_map/ppermute | solution.py:38
  31.7 20.9 %collective-permute-start.3 = (f32[512,256]{1,0:T(8,128)S(1)}, f32[512,256]{1,0:T(8,128)S(1)}, u32[]{:S(2)}, u32[]{:S(2)}) collective-permute-start(f32[512,256]{1,0:T(8,128)S(1)} %get-tuple-element.33), channel_id=1, source_target_pairs={{0,8},{8,16},{16,24},{24,32},{32,40},{40,48},{48,56},{56,64},{64,7... | collective-permute-start | bytes 1572872 | tf_op jit(solution)/shard_map/ppermute | solution.py:38
  43.5 20.3 %collective-permute-start.2 = (f32[512,256]{1,0:T(8,128)S(1)}, f32[512,256]{1,0:T(8,128)S(1)}, u32[]{:S(2)}, u32[]{:S(2)}) collective-permute-start(f32[512,256]{1,0:T(8,128)S(1)} %get-tuple-element.32), channel_id=1, source_target_pairs={{0,8},{8,16},{16,24},{24,32},{32,40},{40,48},{48,56},{56,64},{64,7... | collective-permute-start | bytes 1572872 | tf_op jit(solution)/shard_map/ppermute | solution.py:38
  65.5 4.7 %collective-permute-start.4 = (f32[4,128,256]{2,1,0:T(8,128)S(1)}, f32[4,128,256]{2,1,0:T(8,128)S(1)}, u32[]{:S(2)}, u32[]{:S(2)}) collective-permute-start(f32[4,128,256]{2,1,0:T(8,128)S(1)} %get-tuple-element.39), channel_id=1, source_target_pairs={{0,1},{1,0},{2,3},{3,2},{4,5},{5,4},{6,7},{7,6},{8,9},{9,8},{10,11... | collective-permute-start | bytes 1572872 | tf_op jit(solution)/shard_map/ppermute | solution.py:246
  71.0 12.9 %all-to-all-start = ((f32[4,128,256]{2,1,0:T(8,128)}), f32[4,128,256]{2,1,0:T(8,128)S(1)}, u32[]{:S(2)}, u32[]{:S(2)}) async-start(f32[4,128,256]{2,1,0:T(8,128)} %add.3), calls=%async_computation | async-start | bytes 1048576 | tf_op jit(solution)/shard_map/all_to_all | solution.py:252

commit v3 on v0

v3 whole, which is shorter than its diff:
```python
import functools

import jax
import jax.numpy as jnp
from jax import lax
from jax.experimental import pallas as pl
from jax.experimental.pallas import tpu as pltpu
from jax.sharding import PartitionSpec as P

R = 256
TILE = 128
STEPS = 3
ROW_TILES = 8
COL_TILES = 8
SLOTS = 24
ROWS = ROW_TILES * TILE
COLS = COL_TILES * TILE
WIDE = 2 * TILE
PARTS = ((0, 4), (4, 4))


learn_rate = 0.05
weight_decay = 0.02
user_scale = 1.0 / 64.0

CORE_GROUPS = [[0, 2, 4, 6], [1, 3, 5, 7]]

vmem = pl.BlockSpec(memory_space=pltpu.VMEM)
anywhere = pl.BlockSpec(memory_space=pl.ANY)
contract_last = (((1,), (1,)), ((), ()))
contract_first = (((0,), (0,)), ((), ()))


def passed_along(value, axis, steps):
    count = lax.axis_size(axis)
    pairs = [(source, (source + steps) % count) for source in range(count)]
    return lax.ppermute(value, axis, pairs)


def in_hbm(array):
    return pltpu.with_memory_space_constraint(array, pltpu.HBM)


def start_lists(ids_hbm, count_hbm, ids_ref, count_ref, ids_sem, count_sem):
    copies = [
        pltpu.make_async_copy(ids_hbm, ids_ref, ids_sem),
        pltpu.make_async_copy(count_hbm, count_ref, count_sem),
    ]
    for copy in copies:
        copy.start()
    return copies


def find_slots(step, ids_ref, count_ref, slot_ref):
    for tile in range(ROW_TILES * COL_TILES):
        slot_ref[tile] = -1
    live_count = count_ref[0, 0, step]
    for slot in range(SLOTS):
        slot_ref[ids_ref[step, 0, slot]] = jnp.where(slot < live_count, slot, -1)


def fill_residual(part, users_ref, rounded_ref, rating_ref, slot_ref, residual_ref, before_ratings):
    first_col, tiles = part
    width = min(WIDE, tiles * TILE)
    for wide in range(tiles * TILE // width):
        cols = slice(wide * width, (wide + 1) * width)
        for block in range(ROWS // WIDE):
            rows = slice(block * WIDE, (block + 1) * WIDE)
            predicted = lax.dot_general(
                users_ref[rows, :], rounded_ref[cols, :], contract_last, preferred_element_type=jnp.float32
            )
            if wide == 0 and block == 0:
                before_ratings()
            for down in range(2):
                for across in range(width // TILE):
                    tile_row = block * 2 + down
                    tile_col = first_col + wide * (width // TILE) + across
                    slot = slot_ref[tile_row * COL_TILES + tile_col]
                    rating = rating_ref[jnp.maximum(slot, 0)].astype(jnp.float32)
                    piece = predicted[down * TILE:(down + 1) * TILE, across * TILE:(across + 1) * TILE]
                    piece = jnp.where(slot >= 0, piece - rating, 0.0).astype(jnp.bfloat16)
                    residual_ref[
                        tile_row * TILE:(tile_row + 1) * TILE,
                        wide * width + across * TILE:wide * width + (across + 1) * TILE,
                    ] = piece


def update_panel(part, users_ref, panel_ref, residual_ref, new_ref):
    width = min(WIDE, part[1] * TILE)
    for wide in range(part[1] * TILE // width):
        cols = slice(wide * width, (wide + 1) * width)
        item_grad = lax.dot_general(
            residual_ref[:, cols], users_ref[...], contract_first, preferred_element_type=jnp.float32
        )
        held = panel_ref[cols, :]
        new_ref[cols, :] = held - learn_rate * (item_grad + weight_decay * held)


def first_kernel(part, ids_hbm, count_hbm, users_hbm, panel_hbm, rating_hbm,
                 new_ref, residual_ref, rounded_ref, users_ref, rating_ref,
                 slot_ref, ids_ref, count_ref, ids_sem, count_sem, panel_ref, users_sem, panel_sem, rating_sem):
    lists = start_lists(ids_hbm, count_hbm, ids_ref, count_ref, ids_sem, count_sem)
    panel_copy = pltpu.make_async_copy(
        panel_hbm.at[pl.ds(part[0] * TILE, part[1] * TILE)], panel_ref, panel_sem
    )
    users_copy = pltpu.make_async_copy(users_hbm, users_ref, users_sem)
    rating_copy = pltpu.make_async_copy(rating_hbm.at[0], rating_ref, rating_sem)
    panel_copy.start()
    users_copy.start()
    rating_copy.start()
    for copy in lists:
        copy.wait()
    find_slots(0, ids_ref, count_ref, slot_ref)
    panel_copy.wait()
    rounded_ref[...] = panel_ref[...].astype(jnp.bfloat16)
    users_copy.wait()
    fill_residual(part, users_ref, rounded_ref, rating_ref, slot_ref, residual_ref, rating_copy.wait)
    update_panel(part, users_ref, panel_ref, residual_ref, new_ref)


def opening_kernel(part, prefetch, *refs):
    refs = list(refs)
    ids_hbm, count_hbm, users_ref, panel_hbm, rating_ref = refs[:5]
    del refs[:5]
    rating_hbm = refs.pop(0) if prefetch else None
    new_ref, residual_ref, rounded_ref = refs[:3]
    del refs[:3]
    later_ref = refs.pop(0) if prefetch else None
    slot_ref, ids_ref, count_ref, ids_sem, count_sem, panel_ref, panel_sem = refs[:7]
    lists = start_lists(ids_hbm, count_hbm, ids_ref, count_ref, ids_sem, count_sem)
    panel_copy = pltpu.make_async_copy(
        panel_hbm.at[pl.ds(part[0] * TILE, part[1] * TILE)], panel_ref, panel_sem
    )
    panel_copy.start()
    if prefetch:
        later_copy = pltpu.make_async_copy(rating_hbm.at[pl.ds(1, STEPS - 1)], later_ref, refs[7])
        later_copy.start()
    for copy in lists:
        copy.wait()
    find_slots(0, ids_ref, count_ref, slot_ref)
    panel_copy.wait()
    rounded_ref[...] = panel_ref[...].astype(jnp.bfloat16)
    fill_residual(part, users_ref, rounded_ref, rating_ref, slot_ref, residual_ref, lambda: None)
    update_panel(part, users_ref, panel_ref, residual_ref, new_ref)
    if prefetch:
        later_copy.wait()


def residual_stage(step, part, lists_hbm, users_ref, panel_ref, rating_ref, residual_ref, rounded_ref, scratch):
    slot_ref, ids_ref, count_ref, ids_sem, count_sem = scratch
    lists = start_lists(*lists_hbm, ids_ref, count_ref, ids_sem, count_sem)
    rounded_ref[...] = panel_ref[...].astype(jnp.bfloat16)

    def lists_ready():
        for copy in lists:
            copy.wait()
        find_slots(step, ids_ref, count_ref, slot_ref)

    fill_residual(
        part, users_ref, rounded_ref, rating_ref.at[step - 1], slot_ref, residual_ref, lists_ready
    )


def step_kernel(step, part, ids_hbm, count_hbm, users_ref, panel_ref, rating_ref,
                new_ref, residual_ref, rounded_ref, *scratch):
    residual_stage(
        step, part, (ids_hbm, count_hbm), users_ref, panel_ref, rating_ref, residual_ref, rounded_ref, scratch
    )
    update_panel(part, users_ref, panel_ref, residual_ref, new_ref)


def sum_kernel(count, has_total, *refs):
    blocks = list(zip(refs[:count], refs[count:2 * count]))
    total_ref = refs[2 * count] if has_total else None
    out_ref = refs[-1]
    for block in range(ROWS // WIDE):
        rows = slice(block * WIDE, (block + 1) * WIDE)
        value = total_ref[rows, :] if has_total else None
        for residual_ref, rounded_ref in blocks:
            term = jnp.dot(residual_ref[rows, :], rounded_ref[...], preferred_element_type=jnp.float32)
            value = term if value is None else value + term
        out_ref[rows, :] = value


def share_sums(own, residual_ref, rounded_ref, total_ref, out_ref):
    for index in range(ROW_TILES // 2):
        rows = pl.ds(pl.multiple_of((2 * index + own) * TILE, TILE), TILE)
        term = jnp.dot(residual_ref[rows, :], rounded_ref[...], preferred_element_type=jnp.float32)
        out_ref[index] = (term + total_ref[rows, :]) * user_scale


def last_kernel(step, part, ids_hbm, count_hbm, users_ref, panel_ref, rating_ref, total_ref,
                residual_ref, rounded_ref, theirs_ref, *scratch):
    residual_stage(
        step, part, (ids_hbm, count_hbm), users_ref, panel_ref, rating_ref, residual_ref, rounded_ref, scratch
    )
    core = lax.axis_index("item") % 2
    share_sums(1 - core, residual_ref, rounded_ref, total_ref, theirs_ref)


def finish_kernel(part, count, users_ref, panel_ref, residual_ref, rounded_ref, total_ref, *refs):
    placed_refs = refs[:count]
    mine_ref, new_ref = refs[count:]
    core = lax.axis_index("item") % 2
    share_sums(core, residual_ref, rounded_ref, total_ref, mine_ref)
    for (first_col, tiles), placed_ref in zip(PARTS, placed_refs):
        new_ref[first_col * TILE:(first_col + tiles) * TILE, :] = placed_ref[...]
    update_panel(
        part, users_ref, panel_ref, residual_ref, new_ref.at[pl.ds(part[0] * TILE, part[1] * TILE)]
    )


def floats(*shape):
    return jax.ShapeDtypeStruct(shape, jnp.float32)


def rounded(*shape):
    return jax.ShapeDtypeStruct(shape, jnp.bfloat16)


def part_shapes(part):
    width = part[1] * TILE
    return (floats(width, R), rounded(ROWS, width), rounded(width, R))


LISTS = [
    pltpu.SMEM((ROW_TILES * COL_TILES,), jnp.int32),
    pltpu.SMEM((STEPS, 1, SLOTS), jnp.int32),
    pltpu.SMEM((1, 1, STEPS), jnp.int32),
    pltpu.SemaphoreType.DMA,
    pltpu.SemaphoreType.DMA,
]
ROW_SUM = floats(ROWS, R)
QUARTERS = floats(ROW_TILES // 2, TILE, R)


def kernel_call(body, name, work, operands, in_specs, out_shape, scratch, aliases=None):
    return pl.pallas_call(
        body,
        in_specs=in_specs,
        out_specs=jax.tree.map(lambda _: vmem, out_shape),
        out_shape=out_shape,
        scratch_shapes=scratch,
        input_output_aliases=aliases or {},
        compiler_params=pltpu.CompilerParams(vmem_limit_bytes=16 << 20),
        cost_estimate=pl.CostEstimate(
            flops=work * 2 * ROWS * TILE * R, bytes_accessed=work << 18, transcendentals=0
        ),
        name=name,
    )(*operands)


def shards(user_factors, item_panels, ratings, tile_ids, tile_count):
    lists = [in_hbm(tile_ids.transpose(0, 2, 1)), in_hbm(tile_count.transpose(1, 2, 0))]
    list_specs = [anywhere] * 2
    final = len(PARTS) - 1
    panel_hbm = in_hbm(item_panels)
    rating_hbm = in_hbm(ratings)
    moved = []
    blocks = []
    for index, part in enumerate(PARTS):
        panel_scratch = [pltpu.VMEM((part[1] * TILE, R), jnp.float32)]
        if index == 0:
            new, residual, rounded_part, users, rating_now = kernel_call(
                functools.partial(first_kernel, part), "first", 2 * part[1],
                lists + [in_hbm(user_factors), panel_hbm, rating_hbm], list_specs + [anywhere] * 3,
                part_shapes(part) + (rounded(ROWS, R), rounded(SLOTS, TILE, TILE)),
                LISTS + panel_scratch + [pltpu.SemaphoreType.DMA] * 3,
            )
        else:
            prefetch = index == 1
            operands = lists + [users, panel_hbm, rating_now]
            specs = list_specs + [vmem, anywhere, vmem]
            shapes = part_shapes(part)
            if prefetch:
                operands.append(rating_hbm)
                specs.append(anywhere)
                shapes = shapes + (rounded(STEPS - 1, SLOTS, TILE, TILE),)
            results = kernel_call(
                functools.partial(opening_kernel, part, prefetch), "opening_%d" % index, 2 * part[1],
                operands, specs, shapes, LISTS + panel_scratch + [pltpu.SemaphoreType.DMA] * (1 + prefetch),
            )
            new, residual, rounded_part = results[:3]
            if prefetch:
                rating_later = results[3]
        moved.append(passed_along(new, "user", 1))
        blocks.append((residual, rounded_part))

    def add_parts(name, blocks, total):
        operands = [pair[0] for pair in blocks] + [pair[1] for pair in blocks]
        aliases = {}
        if total is not None:
            aliases = {len(operands): 0}
            operands.append(total)
        return kernel_call(
            functools.partial(sum_kernel, len(blocks), total is not None), name, COL_TILES,
            operands, [vmem] * len(operands), ROW_SUM, [], aliases,
        )

    total = add_parts("sum_0", blocks, None)
    for step in range(1, STEPS):
        pieces, moved, blocks = moved, [], []
        for index, part in enumerate(PARTS):
            if step == STEPS - 1 and index == final:
                break
            new, residual, rounded_part = kernel_call(
                functools.partial(step_kernel, step, part), "step_%d_%d" % (step, index), 2 * part[1],
                lists + [users, pieces[index], rating_later], list_specs + [vmem] * 3,
                part_shapes(part), LISTS,
            )
            moved.append(passed_along(new, "user", 1) if step < STEPS - 1 else new)
            blocks.append((residual, rounded_part))
        total = add_parts("sum_%d" % step, blocks, total)
    part = PARTS[final]
    width = part[1] * TILE
    residual, rounded_part, theirs = kernel_call(
        functools.partial(last_kernel, STEPS - 1, part), "last", 2 * part[1],
        lists + [users, pieces[final], rating_later, total], list_specs + [vmem] * 4,
        (rounded(ROWS, width), rounded(width, R), QUARTERS), LISTS,
    )
    pairs = [(source, source ^ 1) for source in range(lax.axis_size("item"))]
    received = lax.ppermute(theirs, "item", pairs)
    mine, panels = kernel_call(
        functools.partial(finish_kernel, part, final), "finish", 2 * part[1],
        [users, pieces[final], residual, rounded_part, total] + moved, [vmem] * (5 + final),
        (QUARTERS, floats(COLS, R)), [],
    )
    spread = lax.all_to_all(mine + received, "item", 0, 0, axis_index_groups=CORE_GROUPS)
    return (panels, jnp.sum(spread, axis=0))


def solution(mesh):
    in_specs = (
        P("user", None),
        P(("user", "item"), None),
        P(None, "user", "item", None),
        P(None, "user", "item"),
        P(None, "user", "item"),
    )
    out_specs = (P(("user", "item"), None), P(("user", "item"), None))
    return jax.shard_map(shards, mesh=mesh, in_specs=in_specs, out_specs=out_specs, check_vma=False)
```

time: 155 us -> 82.9 us (0.53)
  waiting for transfers between devices: 76.2 us -> 39.4 us
  matrix products: 31.8 us -> 0 us
  local copies, waits for them, and re-layouts: 14.4 us -> 0 us
  Pallas kernels: 0 us -> 13.9 us
  between operations: 14.4 us -> 0.75 us
  blocking collectives: 0 us -> 12.8 us
  other arithmetic: 10.4 us -> 0.76 us
  starting transfers between devices: 6.62 us -> 14.9 us
    dot_general x15 -> x0, matrix products: 31.8 us -> none  [the longest x3 9.76 us: padded_update(): jnp.einsum('ka,kir->air', row_pick, user_parts, precision=lax.Precision.H...]
    reduce_scatter x1 -> x0, waiting for transfers between devices: 26.8 us -> none  [shards(): lax.psum_scatter(total_grad, 'item', scatter_dimension=0, tiled=True)]
    pallas_call x0 -> x10, Pallas kernels: none -> 13.9 us  [kernel_call(): pl.pallas_call(body, in_specs=in_specs, out_specs=jax.tree.map(lambda _:...]
    all_to_all x0 -> x1, blocking collectives: none -> 12.8 us  [shards(): lax.all_to_all(mine + received, 'item', 0, 0, axis_index_groups=CORE_GROUPS)]
    ppermute x2 -> x4, waiting for transfers between devices: 49.3 us -> 39.4 us  [passed_along(): return lax.ppermute(value, axis, pairs)]
    gather x6 -> x0, local copies, waits for them, and re-layouts: 8.68 us -> none  [the longest x3 4.37 us: padded_update(): item_block.astype(jnp.bfloat16).reshape(col_tiles, TILE, R)[col_index]]
    ppermute x2 -> x4, starting transfers between devices: 6.59 us -> 11.8 us  [passed_along(): return lax.ppermute(value, axis, pairs)]
    convert_element_type x6 -> x0, other arithmetic: 4.48 us -> none  [the longest x3 2.61 us: padded_update(): item_block.astype(jnp.bfloat16).reshape(col_tiles, TILE, R)[col_index]]
  transfers between devices with their start and end apart: 3 -> 5, of which waited for: 3 -> 4; matrix products, arithmetic and copies ran while one was open for 10% -> 0% of each run, Pallas kernels for 0% -> 12%
where the time goes in v3:
time: 82.9 us; the launch traced here: 82.5 us
  waiting for transfers between devices  39.4 us (48%)
  starting transfers between devices  14.9 us (18%)
  Pallas kernels  13.9 us (17%)
  blocking collectives  12.8 us (15%)
    ppermute x4, waiting for transfers between devices, passed_along(): return lax.ppermute(value, axis, pairs)  39.4 us
    pallas_call x10, Pallas kernels, kernel_call(): pl.pallas_call(body, in_specs=in_specs, out_specs=jax.tree.map(lambda _:...  13.9 us
    all_to_all x1, blocking collectives, shards(): lax.all_to_all(mine + received, 'item', 0, 0, axis_index_groups=CORE_GROUPS)  12.8 us
    ppermute x4, starting transfers between devices, passed_along(): return lax.ppermute(value, axis, pairs)  11.8 us
    ppermute x1, starting transfers between devices, shards(): received = lax.ppermute(theirs, 'item', pairs)  3.16 us
  transfers between devices with their start and end apart: 5, of which 4 were waited for; matrix products, arithmetic and copies ran while one was open for 0% of the time, Pallas kernels for 12%

profile of v3, /device:TPU:1, one launch (start us, length us, event | category | flops | bytes accessed | tf_op | source)
XLA Modules:
  0.0 82.5 jit_solution(4946885878431236121)
XLA Ops:
  0.6 2.3 %first.1 = (f32[512,256]{1,0:T(8,128)S(1)}, bf16[1024,512]{1,0:T(8,128)(2,1)S(1)}, bf16[512,256]{1,0:T(8,128)(2,1)S(1)}, bf16[1024,256]{1,0:T(8,128)(2,1)S(1)}, bf16[24,128,128]{2,1,0:T(8,128)(2,1)S(1)}) custom-call(s32[3,1,24]{2,1,0:T(1,128)} %bitcast.2, s32[1,1,3]{2,1,0:T(1,128)} %bitcast.8, bf16[1024,256]{1,0:T(8,128)(2,1)} %users_hbm.1, ...), custom_call_target="tpu_custom_call" | custom-call | flops 536870912 | bytes 2097152 | tf_op jit(solution)/shard_map/first/pallas_call | solution.py:238
  3.0 4.4 %collective-permute-start.2 = (f32[512,256]{1,0:T(8,128)S(1)}, f32[512,256]{1,0:T(8,128)S(1)}, u32[]{:S(2)}, u32[]{:S(2)}) collective-permute-start(f32[512,256]{1,0:T(8,128)S(1)} %get-tuple-element.30), channel_id=1, source_target_pairs={{0,8},{8,16},{16,24},{24,32},{32,40},{40,48},{48,56},{56,64},{64,7... | collective-permute-start | bytes 1572872 | tf_op jit(solution)/shard_map/ppermute | solution.py:37
  7.3 2.0 %opening_1.1 = (f32[512,256]{1,0:T(8,128)S(1)}, bf16[1024,512]{1,0:T(8,128)(2,1)S(1)}, bf16[512,256]{1,0:T(8,128)(2,1)S(1)}, bf16[2,24,128,128]{3,2,1,0:T(8,128)(2,1)S(1)}) custom-call(s32[3,1,24]{2,1,0:T(1,128)} %bitcast.3, s32[1,1,3]{2,1,0:T(1,128)} %bitcast.9, bf16[1024,256]{1,0:T(8,128)(2,1)S(1)} %get-tuple-element.25.refs_2_.users_ref, ...), custom_call_target="tpu_custom_call" | custom-call | flops 536870912 | bytes 2097152 | tf_op jit(solution)/shard_map/opening_1/pallas_call | solution.py:238
  9.3 3.5 %collective-permute-start = (f32[512,256]{1,0:T(8,128)S(1)}, f32[512,256]{1,0:T(8,128)S(1)}, u32[]{:S(2)}, u32[]{:S(2)}) collective-permute-start(f32[512,256]{1,0:T(8,128)S(1)} %get-tuple-element.27), channel_id=1, source_target_pairs={{0,8},{8,16},{16,24},{24,32},{32,40},{40,48},{48,56},{56,64},{64,7... | collective-permute-start | bytes 1572872 | tf_op jit(solution)/shard_map/ppermute | solution.py:37
  12.9 16.1 %collective-permute-done.2.panel_ref = f32[512,256]{1,0:T(8,128)S(1)} collective-permute-done((f32[512,256]{1,0:T(8,128)S(1)}, f32[512,256]{1,0:T(8,128)S(1)}, u32[]{:S(2)}, u32[]{:S(2)}) %collective-permute-start.2) | collective-permute-done | bytes 524320 | tf_op jit(solution)/shard_map/ppermute | solution.py:37
  29.0 1.5 %step_1_0.1 = (f32[512,256]{1,0:T(8,128)S(1)}, bf16[1024,512]{1,0:T(8,128)(2,1)S(1)}, bf16[512,256]{1,0:T(8,128)(2,1)S(1)}) custom-call(s32[3,1,24]{2,1,0:T(1,128)} %bitcast.4, s32[1,1,3]{2,1,0:T(1,128)} %bitcast.10, bf16[1024,256]{1,0:T(8,128)(2,1)S(1)} %get-tuple-element.25.refs_2_.users_ref, f32[512,256]{1,0:T(8,128)S(1)} %collective-permute-done.2.panel_ref, ...), custom_call_target="tpu_custom_call" | custom-call | flops 536870912 | bytes 2097152 | tf_op jit(solution)/shard_map/step_1_0/pallas_call | solution.py:238
  30.5 1.9 %collective-permute-start.3 = (f32[512,256]{1,0:T(8,128)S(1)}, f32[512,256]{1,0:T(8,128)S(1)}, u32[]{:S(2)}, u32[]{:S(2)}) collective-permute-start(f32[512,256]{1,0:T(8,128)S(1)} %get-tuple-element.31), channel_id=1, source_target_pairs={{0,8},{8,16},{16,24},{24,32},{32,40},{40,48},{48,56},{56,64},{64,7... | collective-permute-start | bytes 1572872 | tf_op jit(solution)/shard_map/ppermute | solution.py:37
  32.4 7.8 %collective-permute-done.panel_ref = f32[512,256]{1,0:T(8,128)S(1)} collective-permute-done((f32[512,256]{1,0:T(8,128)S(1)}, f32[512,256]{1,0:T(8,128)S(1)}, u32[]{:S(2)}, u32[]{:S(2)}) %collective-permute-start) | collective-permute-done | bytes 524320 | tf_op jit(solution)/shard_map/ppermute | solution.py:37
  40.2 1.5 %step_1_1.1 = (f32[512,256]{1,0:T(8,128)S(1)}, bf16[1024,512]{1,0:T(8,128)(2,1)S(1)}, bf16[512,256]{1,0:T(8,128)(2,1)S(1)}) custom-call(s32[3,1,24]{2,1,0:T(1,128)} %bitcast.5, s32[1,1,3]{2,1,0:T(1,128)} %bitcast.11, bf16[1024,256]{1,0:T(8,128)(2,1)S(1)} %get-tuple-element.25.refs_2_.users_ref, f32[512,256]{1,0:T(8,128)S(1)} %collective-permute-done.panel_ref, ...), custom_call_target="tpu_custom_call" | custom-call | flops 536870912 | bytes 2097152 | tf_op jit(solution)/shard_map/step_1_1/pallas_call | solution.py:238
  41.7 1.9 %collective-permute-start.1 = (f32[512,256]{1,0:T(8,128)S(1)}, f32[512,256]{1,0:T(8,128)S(1)}, u32[]{:S(2)}, u32[]{:S(2)}) collective-permute-start(f32[512,256]{1,0:T(8,128)S(1)} %get-tuple-element.29), channel_id=1, source_target_pairs={{0,8},{8,16},{16,24},{24,32},{32,40},{40,48},{48,56},{56,64},{64,7... | collective-permute-start | bytes 1572872 | tf_op jit(solution)/shard_map/ppermute | solution.py:37
  43.7 0.7 sum_0.1.refs_4_
  44.4 0.8 sum_1.1.refs_2_
  45.1 6.3 %collective-permute-done.3.panel_ref = f32[512,256]{1,0:T(8,128)S(1)} collective-permute-done((f32[512,256]{1,0:T(8,128)S(1)}, f32[512,256]{1,0:T(8,128)S(1)}, u32[]{:S(2)}, u32[]{:S(2)}) %collective-permute-start.3) | collective-permute-done | bytes 524320 | tf_op jit(solution)/shard_map/ppermute | solution.py:37
  51.4 1.5 %step_2_0.1 = (f32[512,256]{1,0:T(8,128)S(1)}, bf16[1024,512]{1,0:T(8,128)(2,1)S(1)}, bf16[512,256]{1,0:T(8,128)(2,1)S(1)}) custom-call(s32[3,1,24]{2,1,0:T(1,128)} %bitcast.6, s32[1,1,3]{2,1,0:T(1,128)} %bitcast.12, bf16[1024,256]{1,0:T(8,128)(2,1)S(1)} %get-tuple-element.25.refs_2_.users_ref, f32[512,256]{1,0:T(8,128)S(1)} %collective-permute-done.3.panel_ref, ...), custom_call_target="tpu_custom_call" | custom-call | flops 536870912 | bytes 2097152 | tf_op jit(solution)/shard_map/step_2_0/pallas_call | solution.py:238
  53.0 0.5 sum_2.1.total_ref
  53.4 9.2 %collective-permute-done.1.panel_ref = f32[512,256]{1,0:T(8,128)S(1)} collective-permute-done((f32[512,256]{1,0:T(8,128)S(1)}, f32[512,256]{1,0:T(8,128)S(1)}, u32[]{:S(2)}, u32[]{:S(2)}) %collective-permute-start.1) | collective-permute-done | bytes 524320 | tf_op jit(solution)/shard_map/ppermute | solution.py:37
  62.7 1.5 %last.1 = (bf16[1024,512]{1,0:T(8,128)(2,1)S(1)}, bf16[512,256]{1,0:T(8,128)(2,1)S(1)}, f32[4,128,256]{2,1,0:T(8,128)S(1)}) custom-call(s32[3,1,24]{2,1,0:T(1,128)} %bitcast.7, s32[1,1,3]{2,1,0:T(1,128)} %bitcast.13, bf16[1024,256]{1,0:T(8,128)(2,1)S(1)} %get-tuple-element.25.refs_2_.users_ref, f32[512,256]{1,0:T(8,128)S(1)} %collective-permute-done.1.panel_ref, ...), custom_call_target="tpu_custom_call" | custom-call | flops 536870912 | bytes 2097152 | tf_op jit(solution)/shard_map/last/pallas_call | solution.py:238
  64.2 3.2 %collective-permute-start.4 = (f32[4,128,256]{2,1,0:T(8,128)S(1)}, f32[4,128,256]{2,1,0:T(8,128)S(1)}, u32[]{:S(2)}, u32[]{:S(2)}) collective-permute-start(f32[4,128,256]{2,1,0:T(8,128)S(1)} %get-tuple-element.47), channel_id=1, source_target_pairs={{0,1},{1,0},{2,3},{3,2},{4,5},{5,4},{6,7},{7,6},{8,9},{9,8},{10,11... | collective-permute-start | bytes 1572872 | tf_op jit(solution)/shard_map/ppermute | solution.py:322
  67.4 1.6 %finish.1 = (f32[4,128,256]{2,1,0:T(8,128)S(1)}, f32[1024,256]{1,0:T(8,128)}) custom-call(bf16[1024,256]{1,0:T(8,128)(2,1)S(1)} %get-tuple-element.25.refs_2_.users_ref, f32[512,256]{1,0:T(8,128)S(1)} %collective-permute-done.1.panel_ref, bf16[1024,512]{1,0:T(8,128)(2,1)S(1)} %get-tuple-element.42.residual_ref, ...), custom_call_target="tpu_custom_call" | custom-call | flops 536870912 | bytes 2097152 | tf_op jit(solution)/shard_map/finish/pallas_call | solution.py:238
  69.0 0.0 collective-permute-done.4
  69.0 0.1 add.3
  69.0 12.8 %all_to_all.5 = f32[4,128,256]{2,1,0:T(8,128)S(1)} all-to-all(f32[4,128,256]{2,1,0:T(8,128)S(1)} %add.3), channel_id=1, replica_groups={{0,2,4,6},{1,3,5,7},{8,10,12,14},{9,11,13,15},{16,18,20,22},{17,19,21,2..., dimensions={0} | all-to-all | bytes 1048576 | tf_op jit(solution)/shard_map/all_to_all | solution.py:328
  81.8 0.7 reduce_sum.9
Async XLA Ops:
  3.0 26.0 %collective-permute-start.2 = (f32[512,256]{1,0:T(8,128)S(1)}, f32[512,256]{1,0:T(8,128)S(1)}, u32[]{:S(2)}, u32[]{:S(2)}) collective-permute-start(f32[512,256]{1,0:T(8,128)S(1)} %get-tuple-element.30), channel_id=1, source_target_pairs={{0,8},{8,16},{16,24},{24,32},{32,40},{40,48},{48,56},{56,64},{64,7... | collective-permute-start | bytes 1572872 | tf_op jit(solution)/shard_map/ppermute | solution.py:37
  9.3 30.9 %collective-permute-start = (f32[512,256]{1,0:T(8,128)S(1)}, f32[512,256]{1,0:T(8,128)S(1)}, u32[]{:S(2)}, u32[]{:S(2)}) collective-permute-start(f32[512,256]{1,0:T(8,128)S(1)} %get-tuple-element.27), channel_id=1, source_target_pairs={{0,8},{8,16},{16,24},{24,32},{32,40},{40,48},{48,56},{56,64},{64,7... | collective-permute-start | bytes 1572872 | tf_op jit(solution)/shard_map/ppermute | solution.py:37
  30.5 20.9 %collective-permute-start.3 = (f32[512,256]{1,0:T(8,128)S(1)}, f32[512,256]{1,0:T(8,128)S(1)}, u32[]{:S(2)}, u32[]{:S(2)}) collective-permute-start(f32[512,256]{1,0:T(8,128)S(1)} %get-tuple-element.31), channel_id=1, source_target_pairs={{0,8},{8,16},{16,24},{24,32},{32,40},{40,48},{48,56},{56,64},{64,7... | collective-permute-start | bytes 1572872 | tf_op jit(solution)/shard_map/ppermute | solution.py:37
  41.7 20.9 %collective-permute-start.1 = (f32[512,256]{1,0:T(8,128)S(1)}, f32[512,256]{1,0:T(8,128)S(1)}, u32[]{:S(2)}, u32[]{:S(2)}) collective-permute-start(f32[512,256]{1,0:T(8,128)S(1)} %get-tuple-element.29), channel_id=1, source_target_pairs={{0,8},{8,16},{16,24},{24,32},{32,40},{40,48},{48,56},{56,64},{64,7... | collective-permute-start | bytes 1572872 | tf_op jit(solution)/shard_map/ppermute | solution.py:37
  64.2 4.8 %collective-permute-start.4 = (f32[4,128,256]{2,1,0:T(8,128)S(1)}, f32[4,128,256]{2,1,0:T(8,128)S(1)}, u32[]{:S(2)}, u32[]{:S(2)}) collective-permute-start(f32[4,128,256]{2,1,0:T(8,128)S(1)} %get-tuple-element.47), channel_id=1, source_target_pairs={{0,1},{1,0},{2,3},{3,2},{4,5},{5,4},{6,7},{7,6},{8,9},{9,8},{10,11... | collective-permute-start | bytes 1572872 | tf_op jit(solution)/shard_map/ppermute | solution.py:322

commit v4 on v3

v4 whole, which is shorter than its diff:
```python
import functools

import jax
import jax.numpy as jnp
from jax import lax
from jax.experimental import pallas as pl
from jax.experimental.pallas import tpu as pltpu
from jax.sharding import PartitionSpec as P


R = 256
TILE = 128
STEPS = 3
ROW_TILES = 8
COL_TILES = 8
SLOTS = 24
ROWS = ROW_TILES * TILE
COLS = COL_TILES * TILE
WIDE = 2 * TILE
PARTS = ((0, 2), (2, 4), (6, 2))


learn_rate = 0.05
weight_decay = 0.02
user_scale = 1.0 / 64.0

CORE_GROUPS = [[0, 2, 4, 6], [1, 3, 5, 7]]

smem = pl.BlockSpec(memory_space=pltpu.SMEM)
vmem = pl.BlockSpec(memory_space=pltpu.VMEM)
anywhere = pl.BlockSpec(memory_space=pl.ANY)
contract_last = (((1,), (1,)), ((), ()))
contract_first = (((0,), (0,)), ((), ()))


def passed_along(value, axis, steps):
    count = lax.axis_size(axis)
    pairs = [(source, (source + steps) % count) for source in range(count)]
    return lax.ppermute(value, axis, pairs)


def in_hbm(array):
    return pltpu.with_memory_space_constraint(array, pltpu.HBM)


def row_tile(place):
    return 2 * (place % (ROW_TILES // 2)) + place // (ROW_TILES // 2)


def start_lists(ids_hbm, count_hbm, ids_ref, count_ref, ids_sem, count_sem):
    copies = [
        pltpu.make_async_copy(ids_hbm, ids_ref, ids_sem),
        pltpu.make_async_copy(count_hbm, count_ref, count_sem),
    ]
    for copy in copies:
        copy.start()
    return copies


def find_slots(step, ids_ref, count_ref, slot_ref):
    for tile in range(ROW_TILES * COL_TILES):
        slot_ref[tile] = -1
    live_count = count_ref[0, 0, step]
    for slot in range(SLOTS):
        slot_ref[ids_ref[step, 0, slot]] = jnp.where(slot < live_count, slot, -1)


def fill_residual(part, users_ref, rounded_ref, less_rating, residual_ref, before_ratings=None):
    width = min(WIDE, part[1] * TILE)
    for wide in range(part[1] * TILE // width):
        cols = slice(wide * width, (wide + 1) * width)
        for half in range(2):
            predicted = lax.dot_general(
                users_ref[half].reshape(ROWS // 2, R), rounded_ref[cols, :], contract_last,
                preferred_element_type=jnp.float32,
            )
            if before_ratings is not None:
                before_ratings()
                before_ratings = None
            for down in range(ROW_TILES // 2):
                for across in range(width // TILE):
                    rows = slice(down * TILE, (down + 1) * TILE)
                    col = wide * (width // TILE) + across
                    piece = predicted[rows, across * TILE:(across + 1) * TILE]
                    piece = less_rating(piece, half, down, part[0] + col)
                    residual_ref[half, rows, col * TILE:(col + 1) * TILE] = piece.astype(jnp.bfloat16)


def listed_rating(rating_ref, slot_ref):
    def less_rating(piece, half, down, tile_col):
        slot = slot_ref[row_tile(half * (ROW_TILES // 2) + down) * COL_TILES + tile_col]
        rating = rating_ref[jnp.maximum(slot, 0)].astype(jnp.float32)
        return jnp.where(slot >= 0, piece - rating, 0.0)

    return less_rating


def spread_rating(spread_ref):
    def less_rating(piece, half, down, tile_col):
        rating = spread_ref[
            half, down * TILE:(down + 1) * TILE, tile_col * TILE:(tile_col + 1) * TILE
        ].astype(jnp.float32)
        return jnp.where(rating == rating, piece - rating, 0.0)

    return less_rating


def spread_kernel(step, ids_hbm, count_hbm, rating_ref, spread_ref, slot_ref, ids_ref, count_ref, ids_sem, count_sem):
    for copy in start_lists(ids_hbm, count_hbm, ids_ref, count_ref, ids_sem, count_sem):
        copy.wait()
    find_slots(step, ids_ref, count_ref, slot_ref)
    for half in range(2):
        for down in range(ROW_TILES // 2):
            for col in range(COL_TILES):
                slot = slot_ref[row_tile(half * (ROW_TILES // 2) + down) * COL_TILES + col]
                rating = rating_ref[step - 1, jnp.maximum(slot, 0)]
                spread_ref[half, down * TILE:(down + 1) * TILE, col * TILE:(col + 1) * TILE] = jnp.where(
                    slot >= 0, rating, jnp.array(jnp.nan, jnp.bfloat16)
                )


def update_panel(part, users_ref, panel_ref, residual_ref, new_ref):
    width = min(WIDE, part[1] * TILE)
    for wide in range(part[1] * TILE // width):
        cols = slice(wide * width, (wide + 1) * width)
        item_grad = lax.dot_general(
            residual_ref[:, :, cols].reshape(ROWS, width), users_ref[...].reshape(ROWS, R), contract_first,
            preferred_element_type=jnp.float32,
        )
        held = panel_ref[cols, :]
        new_ref[cols, :] = held - learn_rate * (item_grad + weight_decay * held)


def first_kernel(part, ids_hbm, count_hbm, users_hbm, panel_hbm, rating_hbm,
                 new_ref, residual_ref, rounded_ref, users_ref, rating_ref,
                 slot_ref, ids_ref, count_ref, ids_sem, count_sem, panel_ref, users_sem, panel_sem, rating_sem):
    lists = start_lists(ids_hbm, count_hbm, ids_ref, count_ref, ids_sem, count_sem)
    panel_copy = pltpu.make_async_copy(
        panel_hbm.at[pl.ds(part[0] * TILE, part[1] * TILE)], panel_ref, panel_sem
    )
    users_copies = [
        pltpu.make_async_copy(users_hbm.at[:, half], users_ref.at[half], users_sem.at[half]) for half in range(2)
    ]
    rating_copy = pltpu.make_async_copy(rating_hbm.at[0], rating_ref, rating_sem)
    panel_copy.start()
    for copy in users_copies:
        copy.start()
    rating_copy.start()
    for copy in lists:
        copy.wait()
    find_slots(0, ids_ref, count_ref, slot_ref)
    panel_copy.wait()
    rounded_ref[...] = panel_ref[...].astype(jnp.bfloat16)
    users_copies[0].wait()

    def rest_ready():
        users_copies[1].wait()
        rating_copy.wait()

    fill_residual(part, users_ref, rounded_ref, listed_rating(rating_ref, slot_ref), residual_ref, rest_ready)
    update_panel(part, users_ref, panel_ref, residual_ref, new_ref)


def opening_kernel(part, prefetch, *refs):
    refs = list(refs)
    ids_hbm, count_hbm, users_ref, panel_hbm, rating_ref = refs[:5]
    del refs[:5]
    rating_hbm = refs.pop(0) if prefetch else None
    new_ref, residual_ref, rounded_ref = refs[:3]
    del refs[:3]
    later_ref = refs.pop(0) if prefetch else None
    slot_ref, ids_ref, count_ref, ids_sem, count_sem, panel_ref, panel_sem = refs[:7]
    lists = start_lists(ids_hbm, count_hbm, ids_ref, count_ref, ids_sem, count_sem)
    panel_copy = pltpu.make_async_copy(
        panel_hbm.at[pl.ds(part[0] * TILE, part[1] * TILE)], panel_ref, panel_sem
    )
    panel_copy.start()
    if prefetch:
        later_copy = pltpu.make_async_copy(rating_hbm.at[pl.ds(1, STEPS - 1)], later_ref, refs[7])
        later_copy.start()
    for copy in lists:
        copy.wait()
    find_slots(0, ids_ref, count_ref, slot_ref)
    panel_copy.wait()
    rounded_ref[...] = panel_ref[...].astype(jnp.bfloat16)
    fill_residual(part, users_ref, rounded_ref, listed_rating(rating_ref, slot_ref), residual_ref)
    update_panel(part, users_ref, panel_ref, residual_ref, new_ref)
    if prefetch:
        later_copy.wait()


def step_kernel(part, users_ref, panel_ref, spread_ref, new_ref, residual_ref, rounded_ref):
    rounded_ref[...] = panel_ref[...].astype(jnp.bfloat16)
    fill_residual(part, users_ref, rounded_ref, spread_rating(spread_ref), residual_ref)
    update_panel(part, users_ref, panel_ref, residual_ref, new_ref)


def sum_kernel(count, has_total, *refs):
    blocks = list(zip(refs[:count], refs[count:2 * count]))
    total_ref = refs[2 * count] if has_total else None
    out_ref = refs[-1]
    for half in range(2):
        value = total_ref[half] if has_total else None
        for residual_ref, rounded_ref in blocks:
            term = jnp.dot(residual_ref[half], rounded_ref[...], preferred_element_type=jnp.float32)
            value = term if value is None else value + term
        out_ref[half] = value


def share_sums(own, residual_ref, rounded_ref, total_ref, out_ref):
    term = jnp.dot(residual_ref[own], rounded_ref[...], preferred_element_type=jnp.float32)
    out_ref[...] = (term + total_ref[own]) * user_scale


def last_kernel(part, users_ref, panel_ref, spread_ref, total_ref, residual_ref, rounded_ref, theirs_ref):
    rounded_ref[...] = panel_ref[...].astype(jnp.bfloat16)
    fill_residual(part, users_ref, rounded_ref, spread_rating(spread_ref), residual_ref)
    core = lax.axis_index("item") % 2
    share_sums(1 - core, residual_ref, rounded_ref, total_ref, theirs_ref)


def finish_kernel(part, count, users_ref, panel_ref, residual_ref, rounded_ref, total_ref, *refs):
    placed_refs = refs[:count]
    mine_ref, new_ref = refs[count:]
    core = lax.axis_index("item") % 2
    share_sums(core, residual_ref, rounded_ref, total_ref, mine_ref)
    for (first_col, tiles), placed_ref in zip(PARTS, placed_refs):
        new_ref[first_col * TILE:(first_col + tiles) * TILE, :] = placed_ref[...]
    update_panel(
        part, users_ref, panel_ref, residual_ref, new_ref.at[pl.ds(part[0] * TILE, part[1] * TILE)]
    )


def floats(*shape):
    return jax.ShapeDtypeStruct(shape, jnp.float32)


def rounded(*shape):
    return jax.ShapeDtypeStruct(shape, jnp.bfloat16)


def part_shapes(part):
    width = part[1] * TILE
    return (floats(width, R), rounded(2, ROWS // 2, width), rounded(width, R))


USERS = rounded(2, ROW_TILES // 2, TILE, R)
LISTS = [
    pltpu.SMEM((ROW_TILES * COL_TILES,), jnp.int32),
    pltpu.SMEM((STEPS, 1, SLOTS), jnp.int32),
    pltpu.SMEM((1, 1, STEPS), jnp.int32),
    pltpu.SemaphoreType.DMA,
    pltpu.SemaphoreType.DMA,
]
ROW_SUM = floats(2, ROWS // 2, R)
HALF_SUM = floats(ROWS // 2, R)


def kernel_call(body, work, operands, in_specs, out_shape, scratch, aliases=None):
    return pl.pallas_call(
        body,
        in_specs=in_specs,
        out_specs=jax.tree.map(lambda a: smem if a.dtype == jnp.int32 else vmem, out_shape),
        out_shape=out_shape,
        scratch_shapes=scratch,
        input_output_aliases=aliases or {},
        compiler_params=pltpu.CompilerParams(vmem_limit_bytes=16 << 20),
        cost_estimate=pl.CostEstimate(
            flops=work * 2 * ROWS * TILE * R, bytes_accessed=work << 18, transcendentals=0
        ),
    )(*operands)


def one_device(user_factors, item_panels, ratings, tile_ids, tile_count):
    lists = [in_hbm(tile_ids.transpose(0, 2, 1)), in_hbm(tile_count.transpose(1, 2, 0))]
    list_specs = [anywhere] * 2
    final = len(PARTS) - 1
    panel_hbm = in_hbm(item_panels)
    rating_hbm = in_hbm(ratings)
    moved = []
    blocks = []
    for index, part in enumerate(PARTS):
        panel_scratch = [pltpu.VMEM((part[1] * TILE, R), jnp.float32)]
        if index == 0:
            new, residual, rounded_part, users, rating_now = kernel_call(
                functools.partial(first_kernel, part), 2 * part[1],
                lists + [in_hbm(user_factors.reshape(ROW_TILES // 2, 2, TILE, R)), panel_hbm, rating_hbm], list_specs + [anywhere] * 3,
                part_shapes(part) + (USERS, rounded(SLOTS, TILE, TILE)),
                LISTS + panel_scratch + [pltpu.SemaphoreType.DMA((2,))] + [pltpu.SemaphoreType.DMA] * 2,
            )
        else:
            prefetch = index == 1
            operands = lists + [users, panel_hbm, rating_now]
            specs = list_specs + [vmem, anywhere, vmem]
            shapes = part_shapes(part)
            if prefetch:
                operands.append(rating_hbm)
                specs.append(anywhere)
                shapes = shapes + (rounded(STEPS - 1, SLOTS, TILE, TILE),)
            results = kernel_call(
                functools.partial(opening_kernel, part, prefetch), 2 * part[1],
                operands, specs, shapes, LISTS + panel_scratch + [pltpu.SemaphoreType.DMA] * (1 + prefetch),
            )
            new, residual, rounded_part = results[:3]
            if prefetch:
                rating_later = results[3]
        moved.append(passed_along(new, "user", 1))
        blocks.append((residual, rounded_part))

    def add_parts(blocks, total):
        operands = [pair[0] for pair in blocks] + [pair[1] for pair in blocks]
        aliases = {}
        if total is not None:
            aliases = {len(operands): 0}
            operands.append(total)
        return kernel_call(
            functools.partial(sum_kernel, len(blocks), total is not None), COL_TILES,
            operands, [vmem] * len(operands), ROW_SUM, [], aliases,
        )

    total = add_parts(blocks, None)
    spread = [
        kernel_call(
            functools.partial(spread_kernel, step), 2, lists + [rating_later],
            list_specs + [vmem], rounded(2, ROWS // 2, COLS), LISTS,
        )
        for step in range(1, STEPS)
    ]
    for step in range(1, STEPS):
        pieces, moved, blocks = moved, [], []
        for index, part in enumerate(PARTS):
            if step == STEPS - 1 and index == final:
                break
            new, residual, rounded_part = kernel_call(
                functools.partial(step_kernel, part), 2 * part[1],
                [users, pieces[index], spread[step - 1]], [vmem] * 3, part_shapes(part), [],
            )
            if step < STEPS - 1:
                new = passed_along(new, "user", 1)
            moved.append(new)
            blocks.append((residual, rounded_part))
        total = add_parts(blocks, total)
    part = PARTS[final]
    width = part[1] * TILE
    residual, rounded_part, theirs = kernel_call(
        functools.partial(last_kernel, part), 2 * part[1],
        [users, pieces[final], spread[-1], total], [vmem] * 4,
        (rounded(2, ROWS // 2, width), rounded(width, R), HALF_SUM), [],
    )
    pairs = [(source, source ^ 1) for source in range(lax.axis_size("item"))]
    received = lax.ppermute(theirs, "item", pairs)
    mine, panels = kernel_call(
        functools.partial(finish_kernel, part, final), 2 * part[1],
        [users, pieces[final], residual, rounded_part, total] + moved, [vmem] * (5 + final),
        (HALF_SUM, floats(COLS, R)), [],
    )
    joined = (mine + received).reshape(ROW_TILES // 2, TILE, R)
    shares = lax.all_to_all(joined, "item", 0, 0, axis_index_groups=CORE_GROUPS)
    return (panels, jnp.sum(shares, axis=0))


def solution(mesh):
    in_specs = (
        P("user", None),
        P(("user", "item"), None),
        P(None, "user", "item", None),
        P(None, "user", "item"),
        P(None, "user", "item"),
    )
    out_specs = (P(("user", "item"), None), P(("user", "item"), None))
    return jax.shard_map(one_device, mesh=mesh, in_specs=in_specs, out_specs=out_specs, check_vma=False)
```

time: 82.9 us -> 89.4 us (1.078)
  starting transfers between devices: 14.9 us -> 24.2 us
  waiting for transfers between devices: 39.4 us -> 33.9 us
  Pallas kernels: 13.9 us -> 16.8 us
    ppermute x4 -> x6, waiting for transfers between devices: 39.4 us -> 33.7 us  [passed_along(): return lax.ppermute(value, axis, pairs)]
    ppermute x1, starting transfers between devices: 3.16 us -> 8.6 us  [one_device(): received = lax.ppermute(theirs, 'item', pairs)]
    ppermute x4 -> x6, starting transfers between devices: 11.8 us -> 15.6 us  [passed_along(): return lax.ppermute(value, axis, pairs)]
    pallas_call x10 -> x15, Pallas kernels: 13.9 us -> 16.8 us  [kernel_call(): pl.pallas_call(body, in_specs=in_specs, out_specs=jax.tree.map(lambda a:...]
  transfers between devices with their start and end apart: 5 -> 7, of which waited for: 4 -> 5; matrix products, arithmetic and copies ran while one was open for 0% -> 0% of each run, Pallas kernels for 12% -> 14%
where the time goes in v4:
time: 89.4 us; the launch traced here: 88.9 us
  waiting for transfers between devices  33.9 us (38%)
  starting transfers between devices  24.2 us (27%)
  Pallas kernels  16.8 us (19%)
  blocking collectives  12.4 us (14%)
    ppermute x6, waiting for transfers between devices, passed_along(): return lax.ppermute(value, axis, pairs)  33.7 us
    pallas_call x15, Pallas kernels, kernel_call(): pl.pallas_call(body, in_specs=in_specs, out_specs=jax.tree.map(lambda a:...  16.8 us
    ppermute x6, starting transfers between devices, passed_along(): return lax.ppermute(value, axis, pairs)  15.6 us
    all_to_all x1, blocking collectives, one_device(): shares = lax.all_to_all(joined, 'item', 0, 0, axis_index_groups=CORE_GROUPS)  12.4 us
    ppermute x1, starting transfers between devices, one_device(): received = lax.ppermute(theirs, 'item', pairs)  8.6 us
  transfers between devices with their start and end apart: 7, of which 5 were waited for; matrix products, arithmetic and copies ran while one was open for 0% of the time, Pallas kernels for 14%

profile of v4, /device:TPU:1, one launch (start us, length us, event | category | flops | bytes accessed | tf_op | source)
XLA Modules:
  0.0 88.9 jit_solution(8957529457981425978)
XLA Ops:
  0.6 2.0 %shard_map.68 = (f32[256,256]{1,0:T(8,128)S(1)}, bf16[2,512,256]{2,1,0:T(8,128)(2,1)S(1)}, bf16[256,256]{1,0:T(8,128)(2,1)S(1)}, bf16[2,4,128,256]{3,2,1,0:T(8,128)(2,1)S(1)}, bf16[24,128,128]{2,1,0:T(8,128)(2,1)S(1)}) custom-call(s32[3,1,24]{2,1,0:T(1,128)} %bitcast.6, s32[1,1,3]{2,1,0:T(1,128)} %bitcast.11, bf16[4,2,128,256]{3,2,1,0:T(8,128)(2,1)} %bitcast.5, ...), custom_call_target="tpu_custom_call" | custom-call | flops 268435456 | bytes 1048576 | tf_op jit(solution)/shard_map/pallas_call | solution.py:260
  2.7 2.0 %shard_map.70 = (f32[512,256]{1,0:T(8,128)S(1)}, bf16[2,512,512]{2,1,0:T(8,128)(2,1)S(1)}, bf16[512,256]{1,0:T(8,128)(2,1)S(1)}, bf16[2,24,128,128]{3,2,1,0:T(8,128)(2,1)S(1)}) custom-call(s32[3,1,24]{2,1,0:T(1,128)} %bitcast.7, s32[1,1,3]{2,1,0:T(1,128)} %bitcast.12, bf16[2,4,128,256]{3,2,1,0:T(8,128)(2,1)S(1)} %get-tuple-element.34.refs_2_.users_ref, ...), custom_call_target="tpu_custom_call" | custom-call | flops 536870912 | bytes 2097152 | tf_op jit(solution)/shard_map/pallas_call | solution.py:260
  4.7 4.4 %collective-permute-start.4 = (f32[512,256]{1,0:T(8,128)S(1)}, f32[512,256]{1,0:T(8,128)S(1)}, u32[]{:S(2)}, u32[]{:S(2)}) collective-permute-start(f32[512,256]{1,0:T(8,128)S(1)} %get-tuple-element.42), channel_id=1, source_target_pairs={{0,8},{8,16},{16,24},{24,32},{32,40},{40,48},{48,56},{56,64},{64,7... | collective-permute-start | bytes 1572872 | tf_op jit(solution)/shard_map/ppermute | solution.py:39
  9.1 3.5 %collective-permute-start.2 = (f32[256,256]{1,0:T(8,128)S(1)}, f32[256,256]{1,0:T(8,128)S(1)}, u32[]{:S(2)}, u32[]{:S(2)}) collective-permute-start(f32[256,256]{1,0:T(8,128)S(1)} %get-tuple-element.39), channel_id=1, source_target_pairs={{0,8},{8,16},{16,24},{24,32},{32,40},{40,48},{48,56},{56,64},{64,7... | collective-permute-start | bytes 786440 | tf_op jit(solution)/shard_map/ppermute | solution.py:39
  12.6 1.5 %shard_map.71.spread_ref = bf16[2,512,1024]{2,1,0:T(8,128)(2,1)S(1)} custom-call(s32[3,1,24]{2,1,0:T(1,128)} %bitcast.8, s32[1,1,3]{2,1,0:T(1,128)} %bitcast.13, bf16[2,24,128,128]{3,2,1,0:T(8,128)(2,1)S(1)} %get-tuple-element.37.rating_ref), custom_call_target="tpu_custom_call" | custom-call | flops 134217728 | bytes 524288 | tf_op jit(solution)/shard_map/pallas_call | solution.py:260
  14.1 16.6 %collective-permute-done.4.panel_ref = f32[512,256]{1,0:T(8,128)S(1)} collective-permute-done((f32[512,256]{1,0:T(8,128)S(1)}, f32[512,256]{1,0:T(8,128)S(1)}, u32[]{:S(2)}, u32[]{:S(2)}) %collective-permute-start.4) | collective-permute-done | bytes 524320 | tf_op jit(solution)/shard_map/ppermute | solution.py:39
  30.7 0.9 %shard_map.76 = (f32[512,256]{1,0:T(8,128)S(1)}, bf16[2,512,512]{2,1,0:T(8,128)(2,1)S(1)}, bf16[512,256]{1,0:T(8,128)(2,1)S(1)}) custom-call(bf16[2,4,128,256]{3,2,1,0:T(8,128)(2,1)S(1)} %get-tuple-element.34.refs_2_.users_ref, f32[512,256]{1,0:T(8,128)S(1)} %collective-permute-done.4.panel_ref, bf16[2,512,1024]{2,1,0:T(8,128)(2,1)S(1)} %shard_map.71.spread_ref), custom_call_target="tpu_custom_call" | custom-call | flops 536870912 | bytes 2097152 | tf_op jit(solution)/shard_map/pallas_call | solution.py:260
  31.6 1.9 %collective-permute-start.5 = (f32[512,256]{1,0:T(8,128)S(1)}, f32[512,256]{1,0:T(8,128)S(1)}, u32[]{:S(2)}, u32[]{:S(2)}) collective-permute-start(f32[512,256]{1,0:T(8,128)S(1)} %get-tuple-element.43), channel_id=1, source_target_pairs={{0,8},{8,16},{16,24},{24,32},{32,40},{40,48},{48,56},{56,64},{64,7... | collective-permute-start | bytes 1572872 | tf_op jit(solution)/shard_map/ppermute | solution.py:39
  33.5 1.8 %shard_map.69 = (f32[256,256]{1,0:T(8,128)S(1)}, bf16[2,512,256]{2,1,0:T(8,128)(2,1)S(1)}, bf16[256,256]{1,0:T(8,128)(2,1)S(1)}) custom-call(s32[3,1,24]{2,1,0:T(1,128)} %bitcast.9, s32[1,1,3]{2,1,0:T(1,128)} %bitcast.14, bf16[2,4,128,256]{3,2,1,0:T(8,128)(2,1)S(1)} %get-tuple-element.34.refs_2_.users_ref, f32[1024,256]{1,0:T(8,128)} %refs_3_.3, ...), custom_call_target="tpu_custom_call" | custom-call | flops 268435456 | bytes 1048576 | tf_op jit(solution)/shard_map/pallas_call | solution.py:260
  35.3 1.9 %collective-permute-start = (f32[256,256]{1,0:T(8,128)S(1)}, f32[256,256]{1,0:T(8,128)S(1)}, u32[]{:S(2)}, u32[]{:S(2)}) collective-permute-start(f32[256,256]{1,0:T(8,128)S(1)} %get-tuple-element.36), channel_id=1, source_target_pairs={{0,8},{8,16},{16,24},{24,32},{32,40},{40,48},{48,56},{56,64},{64,7... | collective-permute-start | bytes 786440 | tf_op jit(solution)/shard_map/ppermute | solution.py:39
  37.2 0.0 collective-permute-done.2.panel_ref
  37.2 0.8 shard_map.74
  38.0 1.9 %collective-permute-start.3 = (f32[256,256]{1,0:T(8,128)S(1)}, f32[256,256]{1,0:T(8,128)S(1)}, u32[]{:S(2)}, u32[]{:S(2)}) collective-permute-start(f32[256,256]{1,0:T(8,128)S(1)} %get-tuple-element.40), channel_id=1, source_target_pairs={{0,8},{8,16},{16,24},{24,32},{32,40},{40,48},{48,56},{56,64},{64,7... | collective-permute-start | bytes 786440 | tf_op jit(solution)/shard_map/ppermute | solution.py:39
  39.9 13.9 %collective-permute-done.panel_ref = f32[256,256]{1,0:T(8,128)S(1)} collective-permute-done((f32[256,256]{1,0:T(8,128)S(1)}, f32[256,256]{1,0:T(8,128)S(1)}, u32[]{:S(2)}, u32[]{:S(2)}) %collective-permute-start) | collective-permute-done | bytes 262176 | tf_op jit(solution)/shard_map/ppermute | solution.py:39
  53.8 0.8 shard_map.72
  54.6 1.9 %collective-permute-start.1 = (f32[256,256]{1,0:T(8,128)S(1)}, f32[256,256]{1,0:T(8,128)S(1)}, u32[]{:S(2)}, u32[]{:S(2)}) collective-permute-start(f32[256,256]{1,0:T(8,128)S(1)} %get-tuple-element.38), channel_id=1, source_target_pairs={{0,8},{8,16},{16,24},{24,32},{32,40},{40,48},{48,56},{56,64},{64,7... | collective-permute-start | bytes 786440 | tf_op jit(solution)/shard_map/ppermute | solution.py:39
  56.5 1.5 %shard_map.73.spread_ref = bf16[2,512,1024]{2,1,0:T(8,128)(2,1)S(1)} custom-call(s32[3,1,24]{2,1,0:T(1,128)} %bitcast.10, s32[1,1,3]{2,1,0:T(1,128)} %bitcast.15, bf16[2,24,128,128]{3,2,1,0:T(8,128)(2,1)S(1)} %get-tuple-element.37.rating_ref), custom_call_target="tpu_custom_call" | custom-call | flops 134217728 | bytes 524288 | tf_op jit(solution)/shard_map/pallas_call | solution.py:260
  58.0 0.7 shard_map.78.refs_6_
  58.7 0.7 collective-permute-done.3.panel_ref
  59.4 0.8 shard_map.75
  60.2 0.7 shard_map.79.refs_4_
  60.9 0.0 collective-permute-done.5.panel_ref
  60.9 0.9 %shard_map.77 = (f32[512,256]{1,0:T(8,128)S(1)}, bf16[2,512,512]{2,1,0:T(8,128)(2,1)S(1)}, bf16[512,256]{1,0:T(8,128)(2,1)S(1)}) custom-call(bf16[2,4,128,256]{3,2,1,0:T(8,128)(2,1)S(1)} %get-tuple-element.34.refs_2_.users_ref, f32[512,256]{1,0:T(8,128)S(1)} %collective-permute-done.5.panel_ref, bf16[2,512,1024]{2,1,0:T(8,128)(2,1)S(1)} %shard_map.73.spread_ref), custom_call_target="tpu_custom_call" | custom-call | flops 536870912 | bytes 2097152 | tf_op jit(solution)/shard_map/pallas_call | solution.py:260
  61.8 0.6 shard_map.80.total_ref
  62.4 2.6 %collective-permute-done.1.panel_ref = f32[256,256]{1,0:T(8,128)S(1)} collective-permute-done((f32[256,256]{1,0:T(8,128)S(1)}, f32[256,256]{1,0:T(8,128)S(1)}, u32[]{:S(2)}, u32[]{:S(2)}) %collective-permute-start.1) | collective-permute-done | bytes 262176 | tf_op jit(solution)/shard_map/ppermute | solution.py:39
  65.0 0.6 shard_map.81
  65.6 8.6 %collective-permute-start.6 = (f32[512,256]{1,0:T(8,128)S(1)}, f32[512,256]{1,0:T(8,128)S(1)}, u32[]{:S(2)}, u32[]{:S(2)}) collective-permute-start(f32[512,256]{1,0:T(8,128)S(1)} %get-tuple-element.65), channel_id=1, source_target_pairs={{0,1},{1,0},{2,3},{3,2},{4,5},{5,4},{6,7},{7,6},{8,9},{9,8},{10,11... | collective-permute-start | bytes 1572872 | tf_op jit(solution)/shard_map/ppermute | solution.py:351
  74.2 1.4 %shard_map.82 = (f32[512,256]{1,0:T(8,128)S(1)}, f32[1024,256]{1,0:T(8,128)}) custom-call(bf16[2,4,128,256]{3,2,1,0:T(8,128)(2,1)S(1)} %get-tuple-element.34.refs_2_.users_ref, f32[256,256]{1,0:T(8,128)S(1)} %collective-permute-done.1.panel_ref, bf16[2,512,256]{2,1,0:T(8,128)(2,1)S(1)} %get-tuple-element.59.residual_ref, ...), custom_call_target="tpu_custom_call" | custom-call | flops 268435456 | bytes 1048576 | tf_op jit(solution)/shard_map/pallas_call | solution.py:260
  75.6 0.1 collective-permute-done.6
  75.7 0.1 add.3
  75.8 12.4 %all_to_all.5 = f32[4,128,256]{2,1,0:T(8,128)S(1)} all-to-all(f32[4,128,256]{2,1,0:T(8,128)S(1)} %bitcast.4), channel_id=1, replica_groups={{0,2,4,6},{1,3,5,7},{8,10,12,14},{9,11,13,15},{16,18,20,22},{17,19,21,2..., dimensions={0} | all-to-all | bytes 1048576 | tf_op jit(solution)/shard_map/all_to_all | solution.py:358
  88.2 0.7 reduce_sum.9
Async XLA Ops:
  4.7 26.0 %collective-permute-start.4 = (f32[512,256]{1,0:T(8,128)S(1)}, f32[512,256]{1,0:T(8,128)S(1)}, u32[]{:S(2)}, u32[]{:S(2)}) collective-permute-start(f32[512,256]{1,0:T(8,128)S(1)} %get-tuple-element.42), channel_id=1, source_target_pairs={{0,8},{8,16},{16,24},{24,32},{32,40},{40,48},{48,56},{56,64},{64,7... | collective-permute-start | bytes 1572872 | tf_op jit(solution)/shard_map/ppermute | solution.py:39
  9.1 28.2 %collective-permute-start.2 = (f32[256,256]{1,0:T(8,128)S(1)}, f32[256,256]{1,0:T(8,128)S(1)}, u32[]{:S(2)}, u32[]{:S(2)}) collective-permute-start(f32[256,256]{1,0:T(8,128)S(1)} %get-tuple-element.39), channel_id=1, source_target_pairs={{0,8},{8,16},{16,24},{24,32},{32,40},{40,48},{48,56},{56,64},{64,7... | collective-permute-start | bytes 786440 | tf_op jit(solution)/shard_map/ppermute | solution.py:39
  31.6 29.3 %collective-permute-start.5 = (f32[512,256]{1,0:T(8,128)S(1)}, f32[512,256]{1,0:T(8,128)S(1)}, u32[]{:S(2)}, u32[]{:S(2)}) collective-permute-start(f32[512,256]{1,0:T(8,128)S(1)} %get-tuple-element.43), channel_id=1, source_target_pairs={{0,8},{8,16},{16,24},{24,32},{32,40},{40,48},{48,56},{56,64},{64,7... | collective-permute-start | bytes 1572872 | tf_op jit(solution)/shard_map/ppermute | solution.py:39
  35.3 18.5 %collective-permute-start = (f32[256,256]{1,0:T(8,128)S(1)}, f32[256,256]{1,0:T(8,128)S(1)}, u32[]{:S(2)}, u32[]{:S(2)}) collective-permute-start(f32[256,256]{1,0:T(8,128)S(1)} %get-tuple-element.36), channel_id=1, source_target_pairs={{0,8},{8,16},{16,24},{24,32},{32,40},{40,48},{48,56},{56,64},{64,7... | collective-permute-start | bytes 786440 | tf_op jit(solution)/shard_map/ppermute | solution.py:39
  38.0 21.4 %collective-permute-start.3 = (f32[256,256]{1,0:T(8,128)S(1)}, f32[256,256]{1,0:T(8,128)S(1)}, u32[]{:S(2)}, u32[]{:S(2)}) collective-permute-start(f32[256,256]{1,0:T(8,128)S(1)} %get-tuple-element.40), channel_id=1, source_target_pairs={{0,8},{8,16},{16,24},{24,32},{32,40},{40,48},{48,56},{56,64},{64,7... | collective-permute-start | bytes 786440 | tf_op jit(solution)/shard_map/ppermute | solution.py:39
  54.6 10.4 %collective-permute-start.1 = (f32[256,256]{1,0:T(8,128)S(1)}, f32[256,256]{1,0:T(8,128)S(1)}, u32[]{:S(2)}, u32[]{:S(2)}) collective-permute-start(f32[256,256]{1,0:T(8,128)S(1)} %get-tuple-element.38), channel_id=1, source_target_pairs={{0,8},{8,16},{16,24},{24,32},{32,40},{40,48},{48,56},{56,64},{64,7... | collective-permute-start | bytes 786440 | tf_op jit(solution)/shard_map/ppermute | solution.py:39
  65.6 10.1 %collective-permute-start.6 = (f32[512,256]{1,0:T(8,128)S(1)}, f32[512,256]{1,0:T(8,128)S(1)}, u32[]{:S(2)}, u32[]{:S(2)}) collective-permute-start(f32[512,256]{1,0:T(8,128)S(1)} %get-tuple-element.65), channel_id=1, source_target_pairs={{0,1},{1,0},{2,3},{3,2},{4,5},{5,4},{6,7},{7,6},{8,9},{9,8},{10,11... | collective-permute-start | bytes 1572872 | tf_op jit(solution)/shard_map/ppermute | solution.py:351

commit v5 on v4

--- a/solution.py
+++ b/solution.py
@@ -65,25 +65,30 @@
         slot_ref[ids_ref[step, 0, slot]] = jnp.where(slot < live_count, slot, -1)
 
 
-def fill_residual(part, users_ref, rounded_ref, less_rating, residual_ref, before_ratings=None):
+def predict(cols, half, users_ref, rounded_ref):
+    return lax.dot_general(
+        users_ref[half].reshape(ROWS // 2, R), rounded_ref[cols, :], contract_last, preferred_element_type=jnp.float32
+    )
+
+
+def take_ratings(part, cols, half, predicted, less_rating, residual_ref):
+    for down in range(ROW_TILES // 2):
+        for col in range(cols.start // TILE, cols.stop // TILE):
+            rows = slice(down * TILE, (down + 1) * TILE)
+            piece = predicted[rows, col * TILE - cols.start:(col + 1) * TILE - cols.start]
+            piece = less_rating(piece, half, down, part[0] + col)
+            residual_ref[half, rows, col * TILE:(col + 1) * TILE] = piece.astype(jnp.bfloat16)
+
+
+def column_blocks(part):
     width = min(WIDE, part[1] * TILE)
-    for wide in range(part[1] * TILE // width):
-        cols = slice(wide * width, (wide + 1) * width)
+    return [slice(start, start + width) for start in range(0, part[1] * TILE, width)]
+
+
+def fill_residual(part, users_ref, rounded_ref, less_rating, residual_ref):
+    for cols in column_blocks(part):
         for half in range(2):
-            predicted = lax.dot_general(
-                users_ref[half].reshape(ROWS // 2, R), rounded_ref[cols, :], contract_last,
-                preferred_element_type=jnp.float32,
-            )
-            if before_ratings is not None:
-                before_ratings()
-                before_ratings = None
-            for down in range(ROW_TILES // 2):
-                for across in range(width // TILE):
-                    rows = slice(down * TILE, (down + 1) * TILE)
-                    col = wide * (width // TILE) + across
-                    piece = predicted[rows, across * TILE:(across + 1) * TILE]
-                    piece = less_rating(piece, half, down, part[0] + col)
-                    residual_ref[half, rows, col * TILE:(col + 1) * TILE] = piece.astype(jnp.bfloat16)
+            take_ratings(part, cols, half, predict(cols, half, users_ref, rounded_ref), less_rating, residual_ref)
 
 
 def listed_rating(rating_ref, slot_ref):
@@ -151,13 +156,13 @@
     find_slots(0, ids_ref, count_ref, slot_ref)
     panel_copy.wait()
     rounded_ref[...] = panel_ref[...].astype(jnp.bfloat16)
-    users_copies[0].wait()
-
-    def rest_ready():
-        users_copies[1].wait()
-        rating_copy.wait()
-
-    fill_residual(part, users_ref, rounded_ref, listed_rating(rating_ref, slot_ref), residual_ref, rest_ready)
+    for copy in users_copies:
+        copy.wait()
+    places = [(cols, half) for cols in column_blocks(part) for half in range(2)]
+    predicted = [predict(cols, half, users_ref, rounded_ref) for cols, half in places]
+    rating_copy.wait()
+    for (cols, half), values in zip(places, predicted):
+        take_ratings(part, cols, half, values, listed_rating(rating_ref, slot_ref), residual_ref)
     update_panel(part, users_ref, panel_ref, residual_ref, new_ref)
 
 

time: 89.4 us -> 89.4 us (level)
  no operation moved by 1% of the time
where the time goes in v5:
time: 89.4 us; the launch traced here: 89 us
  waiting for transfers between devices  33.9 us (38%)
  starting transfers between devices  24.2 us (27%)
  Pallas kernels  16.9 us (19%)
  blocking collectives  12.5 us (14%)
    ppermute x6, waiting for transfers between devices, passed_along(): return lax.ppermute(value, axis, pairs)  33.7 us
    pallas_call x15, Pallas kernels, kernel_call(): pl.pallas_call(body, in_specs=in_specs, out_specs=jax.tree.map(lambda a:...  16.9 us
    ppermute x6, starting transfers between devices, passed_along(): return lax.ppermute(value, axis, pairs)  15.6 us
    all_to_all x1, blocking collectives, one_device(): shares = lax.all_to_all(joined, 'item', 0, 0, axis_index_groups=CORE_GROUPS)  12.5 us
    ppermute x1, starting transfers between devices, one_device(): received = lax.ppermute(theirs, 'item', pairs)  8.59 us
  transfers between devices with their start and end apart: 7, of which 5 were waited for; matrix products, arithmetic and copies ran while one was open for 0% of the time, Pallas kernels for 14%

profile of v5, /device:TPU:1, one launch (start us, length us, event | category | flops | bytes accessed | tf_op | source)
XLA Modules:
  0.0 89.0 jit_solution(5323168864238467922)
XLA Ops:
  0.6 2.1 %shard_map.68 = (f32[256,256]{1,0:T(8,128)S(1)}, bf16[2,512,256]{2,1,0:T(8,128)(2,1)S(1)}, bf16[256,256]{1,0:T(8,128)(2,1)S(1)}, bf16[2,4,128,256]{3,2,1,0:T(8,128)(2,1)S(1)}, bf16[24,128,128]{2,1,0:T(8,128)(2,1)S(1)}) custom-call(s32[3,1,24]{2,1,0:T(1,128)} %bitcast.6, s32[1,1,3]{2,1,0:T(1,128)} %bitcast.11, bf16[4,2,128,256]{3,2,1,0:T(8,128)(2,1)} %bitcast.5, ...), custom_call_target="tpu_custom_call" | custom-call | flops 268435456 | bytes 1048576 | tf_op jit(solution)/shard_map/pallas_call | solution.py:265
  2.8 2.0 %shard_map.70 = (f32[512,256]{1,0:T(8,128)S(1)}, bf16[2,512,512]{2,1,0:T(8,128)(2,1)S(1)}, bf16[512,256]{1,0:T(8,128)(2,1)S(1)}, bf16[2,24,128,128]{3,2,1,0:T(8,128)(2,1)S(1)}) custom-call(s32[3,1,24]{2,1,0:T(1,128)} %bitcast.7, s32[1,1,3]{2,1,0:T(1,128)} %bitcast.12, bf16[2,4,128,256]{3,2,1,0:T(8,128)(2,1)S(1)} %get-tuple-element.34.refs_2_.users_ref, ...), custom_call_target="tpu_custom_call" | custom-call | flops 536870912 | bytes 2097152 | tf_op jit(solution)/shard_map/pallas_call | solution.py:265
  4.8 4.4 %collective-permute-start.4 = (f32[512,256]{1,0:T(8,128)S(1)}, f32[512,256]{1,0:T(8,128)S(1)}, u32[]{:S(2)}, u32[]{:S(2)}) collective-permute-start(f32[512,256]{1,0:T(8,128)S(1)} %get-tuple-element.42), channel_id=1, source_target_pairs={{0,8},{8,16},{16,24},{24,32},{32,40},{40,48},{48,56},{56,64},{64,7... | collective-permute-start | bytes 1572872 | tf_op jit(solution)/shard_map/ppermute | solution.py:39
  9.1 3.6 %collective-permute-start.2 = (f32[256,256]{1,0:T(8,128)S(1)}, f32[256,256]{1,0:T(8,128)S(1)}, u32[]{:S(2)}, u32[]{:S(2)}) collective-permute-start(f32[256,256]{1,0:T(8,128)S(1)} %get-tuple-element.39), channel_id=1, source_target_pairs={{0,8},{8,16},{16,24},{24,32},{32,40},{40,48},{48,56},{56,64},{64,7... | collective-permute-start | bytes 786440 | tf_op jit(solution)/shard_map/ppermute | solution.py:39
  12.7 1.5 %shard_map.71.spread_ref = bf16[2,512,1024]{2,1,0:T(8,128)(2,1)S(1)} custom-call(s32[3,1,24]{2,1,0:T(1,128)} %bitcast.8, s32[1,1,3]{2,1,0:T(1,128)} %bitcast.13, bf16[2,24,128,128]{3,2,1,0:T(8,128)(2,1)S(1)} %get-tuple-element.37.rating_ref), custom_call_target="tpu_custom_call" | custom-call | flops 134217728 | bytes 524288 | tf_op jit(solution)/shard_map/pallas_call | solution.py:265
  14.2 16.6 %collective-permute-done.4.panel_ref = f32[512,256]{1,0:T(8,128)S(1)} collective-permute-done((f32[512,256]{1,0:T(8,128)S(1)}, f32[512,256]{1,0:T(8,128)S(1)}, u32[]{:S(2)}, u32[]{:S(2)}) %collective-permute-start.4) | collective-permute-done | bytes 524320 | tf_op jit(solution)/shard_map/ppermute | solution.py:39
  30.8 0.9 %shard_map.76 = (f32[512,256]{1,0:T(8,128)S(1)}, bf16[2,512,512]{2,1,0:T(8,128)(2,1)S(1)}, bf16[512,256]{1,0:T(8,128)(2,1)S(1)}) custom-call(bf16[2,4,128,256]{3,2,1,0:T(8,128)(2,1)S(1)} %get-tuple-element.34.refs_2_.users_ref, f32[512,256]{1,0:T(8,128)S(1)} %collective-permute-done.4.panel_ref, bf16[2,512,1024]{2,1,0:T(8,128)(2,1)S(1)} %shard_map.71.spread_ref), custom_call_target="tpu_custom_call" | custom-call | flops 536870912 | bytes 2097152 | tf_op jit(solution)/shard_map/pallas_call | solution.py:265
  31.7 1.9 %collective-permute-start.5 = (f32[512,256]{1,0:T(8,128)S(1)}, f32[512,256]{1,0:T(8,128)S(1)}, u32[]{:S(2)}, u32[]{:S(2)}) collective-permute-start(f32[512,256]{1,0:T(8,128)S(1)} %get-tuple-element.43), channel_id=1, source_target_pairs={{0,8},{8,16},{16,24},{24,32},{32,40},{40,48},{48,56},{56,64},{64,7... | collective-permute-start | bytes 1572872 | tf_op jit(solution)/shard_map/ppermute | solution.py:39
  33.6 1.8 %shard_map.69 = (f32[256,256]{1,0:T(8,128)S(1)}, bf16[2,512,256]{2,1,0:T(8,128)(2,1)S(1)}, bf16[256,256]{1,0:T(8,128)(2,1)S(1)}) custom-call(s32[3,1,24]{2,1,0:T(1,128)} %bitcast.9, s32[1,1,3]{2,1,0:T(1,128)} %bitcast.14, bf16[2,4,128,256]{3,2,1,0:T(8,128)(2,1)S(1)} %get-tuple-element.34.refs_2_.users_ref, f32[1024,256]{1,0:T(8,128)} %refs_3_.3, ...), custom_call_target="tpu_custom_call" | custom-call | flops 268435456 | bytes 1048576 | tf_op jit(solution)/shard_map/pallas_call | solution.py:265
  35.4 1.9 %collective-permute-start = (f32[256,256]{1,0:T(8,128)S(1)}, f32[256,256]{1,0:T(8,128)S(1)}, u32[]{:S(2)}, u32[]{:S(2)}) collective-permute-start(f32[256,256]{1,0:T(8,128)S(1)} %get-tuple-element.36), channel_id=1, source_target_pairs={{0,8},{8,16},{16,24},{24,32},{32,40},{40,48},{48,56},{56,64},{64,7... | collective-permute-start | bytes 786440 | tf_op jit(solution)/shard_map/ppermute | solution.py:39
  37.3 0.0 collective-permute-done.2.panel_ref
  37.3 0.8 shard_map.74
  38.1 1.9 %collective-permute-start.3 = (f32[256,256]{1,0:T(8,128)S(1)}, f32[256,256]{1,0:T(8,128)S(1)}, u32[]{:S(2)}, u32[]{:S(2)}) collective-permute-start(f32[256,256]{1,0:T(8,128)S(1)} %get-tuple-element.40), channel_id=1, source_target_pairs={{0,8},{8,16},{16,24},{24,32},{32,40},{40,48},{48,56},{56,64},{64,7... | collective-permute-start | bytes 786440 | tf_op jit(solution)/shard_map/ppermute | solution.py:39
  40.0 13.9 %collective-permute-done.panel_ref = f32[256,256]{1,0:T(8,128)S(1)} collective-permute-done((f32[256,256]{1,0:T(8,128)S(1)}, f32[256,256]{1,0:T(8,128)S(1)}, u32[]{:S(2)}, u32[]{:S(2)}) %collective-permute-start) | collective-permute-done | bytes 262176 | tf_op jit(solution)/shard_map/ppermute | solution.py:39
  53.9 0.8 shard_map.72
  54.7 1.9 %collective-permute-start.1 = (f32[256,256]{1,0:T(8,128)S(1)}, f32[256,256]{1,0:T(8,128)S(1)}, u32[]{:S(2)}, u32[]{:S(2)}) collective-permute-start(f32[256,256]{1,0:T(8,128)S(1)} %get-tuple-element.38), channel_id=1, source_target_pairs={{0,8},{8,16},{16,24},{24,32},{32,40},{40,48},{48,56},{56,64},{64,7... | collective-permute-start | bytes 786440 | tf_op jit(solution)/shard_map/ppermute | solution.py:39
  56.6 1.5 %shard_map.73.spread_ref = bf16[2,512,1024]{2,1,0:T(8,128)(2,1)S(1)} custom-call(s32[3,1,24]{2,1,0:T(1,128)} %bitcast.10, s32[1,1,3]{2,1,0:T(1,128)} %bitcast.15, bf16[2,24,128,128]{3,2,1,0:T(8,128)(2,1)S(1)} %get-tuple-element.37.rating_ref), custom_call_target="tpu_custom_call" | custom-call | flops 134217728 | bytes 524288 | tf_op jit(solution)/shard_map/pallas_call | solution.py:265
  58.1 0.7 shard_map.78.refs_6_
  58.8 0.7 collective-permute-done.3.panel_ref
  59.5 0.8 shard_map.75
  60.3 0.7 shard_map.79.refs_4_
  61.0 0.0 collective-permute-done.5.panel_ref
  61.0 0.9 %shard_map.77 = (f32[512,256]{1,0:T(8,128)S(1)}, bf16[2,512,512]{2,1,0:T(8,128)(2,1)S(1)}, bf16[512,256]{1,0:T(8,128)(2,1)S(1)}) custom-call(bf16[2,4,128,256]{3,2,1,0:T(8,128)(2,1)S(1)} %get-tuple-element.34.refs_2_.users_ref, f32[512,256]{1,0:T(8,128)S(1)} %collective-permute-done.5.panel_ref, bf16[2,512,1024]{2,1,0:T(8,128)(2,1)S(1)} %shard_map.73.spread_ref), custom_call_target="tpu_custom_call" | custom-call | flops 536870912 | bytes 2097152 | tf_op jit(solution)/shard_map/pallas_call | solution.py:265
  61.9 0.6 shard_map.80.total_ref
  62.5 2.6 %collective-permute-done.1.panel_ref = f32[256,256]{1,0:T(8,128)S(1)} collective-permute-done((f32[256,256]{1,0:T(8,128)S(1)}, f32[256,256]{1,0:T(8,128)S(1)}, u32[]{:S(2)}, u32[]{:S(2)}) %collective-permute-start.1) | collective-permute-done | bytes 262176 | tf_op jit(solution)/shard_map/ppermute | solution.py:39
  65.1 0.6 shard_map.81
  65.7 8.6 %collective-permute-start.6 = (f32[512,256]{1,0:T(8,128)S(1)}, f32[512,256]{1,0:T(8,128)S(1)}, u32[]{:S(2)}, u32[]{:S(2)}) collective-permute-start(f32[512,256]{1,0:T(8,128)S(1)} %get-tuple-element.65), channel_id=1, source_target_pairs={{0,1},{1,0},{2,3},{3,2},{4,5},{5,4},{6,7},{7,6},{8,9},{9,8},{10,11... | collective-permute-start | bytes 1572872 | tf_op jit(solution)/shard_map/ppermute | solution.py:356
  74.3 1.4 %shard_map.82 = (f32[512,256]{1,0:T(8,128)S(1)}, f32[1024,256]{1,0:T(8,128)}) custom-call(bf16[2,4,128,256]{3,2,1,0:T(8,128)(2,1)S(1)} %get-tuple-element.34.refs_2_.users_ref, f32[256,256]{1,0:T(8,128)S(1)} %collective-permute-done.1.panel_ref, bf16[2,512,256]{2,1,0:T(8,128)(2,1)S(1)} %get-tuple-element.59.residual_ref, ...), custom_call_target="tpu_custom_call" | custom-call | flops 268435456 | bytes 1048576 | tf_op jit(solution)/shard_map/pallas_call | solution.py:265
  75.7 0.1 collective-permute-done.6
  75.8 0.1 add.3
  75.9 12.5 %all_to_all.5 = f32[4,128,256]{2,1,0:T(8,128)S(1)} all-to-all(f32[4,128,256]{2,1,0:T(8,128)S(1)} %bitcast.4), channel_id=1, replica_groups={{0,2,4,6},{1,3,5,7},{8,10,12,14},{9,11,13,15},{16,18,20,22},{17,19,21,2..., dimensions={0} | all-to-all | bytes 1048576 | tf_op jit(solution)/shard_map/all_to_all | solution.py:363
  88.3 0.7 reduce_sum.9
Async XLA Ops:
  4.8 26.0 %collective-permute-start.4 = (f32[512,256]{1,0:T(8,128)S(1)}, f32[512,256]{1,0:T(8,128)S(1)}, u32[]{:S(2)}, u32[]{:S(2)}) collective-permute-start(f32[512,256]{1,0:T(8,128)S(1)} %get-tuple-element.42), channel_id=1, source_target_pairs={{0,8},{8,16},{16,24},{24,32},{32,40},{40,48},{48,56},{56,64},{64,7... | collective-permute-start | bytes 1572872 | tf_op jit(solution)/shard_map/ppermute | solution.py:39
  9.1 28.2 %collective-permute-start.2 = (f32[256,256]{1,0:T(8,128)S(1)}, f32[256,256]{1,0:T(8,128)S(1)}, u32[]{:S(2)}, u32[]{:S(2)}) collective-permute-start(f32[256,256]{1,0:T(8,128)S(1)} %get-tuple-element.39), channel_id=1, source_target_pairs={{0,8},{8,16},{16,24},{24,32},{32,40},{40,48},{48,56},{56,64},{64,7... | collective-permute-start | bytes 786440 | tf_op jit(solution)/shard_map/ppermute | solution.py:39
  31.7 29.3 %collective-permute-start.5 = (f32[512,256]{1,0:T(8,128)S(1)}, f32[512,256]{1,0:T(8,128)S(1)}, u32[]{:S(2)}, u32[]{:S(2)}) collective-permute-start(f32[512,256]{1,0:T(8,128)S(1)} %get-tuple-element.43), channel_id=1, source_target_pairs={{0,8},{8,16},{16,24},{24,32},{32,40},{40,48},{48,56},{56,64},{64,7... | collective-permute-start | bytes 1572872 | tf_op jit(solution)/shard_map/ppermute | solution.py:39
  35.4 18.5 %collective-permute-start = (f32[256,256]{1,0:T(8,128)S(1)}, f32[256,256]{1,0:T(8,128)S(1)}, u32[]{:S(2)}, u32[]{:S(2)}) collective-permute-start(f32[256,256]{1,0:T(8,128)S(1)} %get-tuple-element.36), channel_id=1, source_target_pairs={{0,8},{8,16},{16,24},{24,32},{32,40},{40,48},{48,56},{56,64},{64,7... | collective-permute-start | bytes 786440 | tf_op jit(solution)/shard_map/ppermute | solution.py:39
  38.1 21.4 %collective-permute-start.3 = (f32[256,256]{1,0:T(8,128)S(1)}, f32[256,256]{1,0:T(8,128)S(1)}, u32[]{:S(2)}, u32[]{:S(2)}) collective-permute-start(f32[256,256]{1,0:T(8,128)S(1)} %get-tuple-element.40), channel_id=1, source_target_pairs={{0,8},{8,16},{16,24},{24,32},{32,40},{40,48},{48,56},{56,64},{64,7... | collective-permute-start | bytes 786440 | tf_op jit(solution)/shard_map/ppermute | solution.py:39
  54.7 10.4 %collective-permute-start.1 = (f32[256,256]{1,0:T(8,128)S(1)}, f32[256,256]{1,0:T(8,128)S(1)}, u32[]{:S(2)}, u32[]{:S(2)}) collective-permute-start(f32[256,256]{1,0:T(8,128)S(1)} %get-tuple-element.38), channel_id=1, source_target_pairs={{0,8},{8,16},{16,24},{24,32},{32,40},{40,48},{48,56},{56,64},{64,7... | collective-permute-start | bytes 786440 | tf_op jit(solution)/shard_map/ppermute | solution.py:39
  65.7 10.1 %collective-permute-start.6 = (f32[512,256]{1,0:T(8,128)S(1)}, f32[512,256]{1,0:T(8,128)S(1)}, u32[]{:S(2)}, u32[]{:S(2)}) collective-permute-start(f32[512,256]{1,0:T(8,128)S(1)} %get-tuple-element.65), channel_id=1, source_target_pairs={{0,1},{1,0},{2,3},{3,2},{4,5},{5,4},{6,7},{7,6},{8,9},{9,8},{10,11... | collective-permute-start | bytes 1572872 | tf_op jit(solution)/shard_map/ppermute | solution.py:356

commit v6 on v5

--- a/solution.py
+++ b/solution.py
@@ -234,6 +234,10 @@
     update_panel(
         part, users_ref, panel_ref, residual_ref, new_ref.at[pl.ds(part[0] * TILE, part[1] * TILE)]
     )
+
+
+def add_shares(shares_ref, out_ref):
+    out_ref[...] = (shares_ref[0] + shares_ref[1]) + (shares_ref[2] + shares_ref[3])
 
 
 def floats(*shape):
@@ -361,7 +365,8 @@
     )
     joined = (mine + received).reshape(ROW_TILES // 2, TILE, R)
     shares = lax.all_to_all(joined, "item", 0, 0, axis_index_groups=CORE_GROUPS)
-    return (panels, jnp.sum(shares, axis=0))
+    share_grad = kernel_call(add_shares, 1, [shares], [vmem], floats(TILE, R), [])
+    return (panels, share_grad)
 
 
 def solution(mesh):

time: 89.4 us -> 89.4 us (level)
    pallas_call x15 -> x16, Pallas kernels: 16.9 us -> 17.6 us  [kernel_call(): pl.pallas_call(body, in_specs=in_specs, out_specs=jax.tree.map(lambda a:...]
where the time goes in v6:
time: 89.4 us; the launch traced here: 89 us
  waiting for transfers between devices  33.9 us (38%)
  starting transfers between devices  24.2 us (27%)
  Pallas kernels  17.6 us (20%)
  blocking collectives  12.4 us (14%)
    ppermute x6, waiting for transfers between devices, passed_along(): return lax.ppermute(value, axis, pairs)  33.7 us
    pallas_call x16, Pallas kernels, kernel_call(): pl.pallas_call(body, in_specs=in_specs, out_specs=jax.tree.map(lambda a:...  17.6 us
    ppermute x6, starting transfers between devices, passed_along(): return lax.ppermute(value, axis, pairs)  15.6 us
    all_to_all x1, blocking collectives, one_device(): shares = lax.all_to_all(joined, 'item', 0, 0, axis_index_groups=CORE_GROUPS)  12.4 us
    ppermute x1, starting transfers between devices, one_device(): received = lax.ppermute(theirs, 'item', pairs)  8.6 us
  transfers between devices with their start and end apart: 7, of which 5 were waited for; matrix products, arithmetic and copies ran while one was open for 0% of the time, Pallas kernels for 14%

profile of v6, /device:TPU:1, one launch (start us, length us, event | category | flops | bytes accessed | tf_op | source)
XLA Modules:
  0.0 89.0 jit_solution(13356358325264465263)
XLA Ops:
  0.6 2.1 %shard_map.68 = (f32[256,256]{1,0:T(8,128)S(1)}, bf16[2,512,256]{2,1,0:T(8,128)(2,1)S(1)}, bf16[256,256]{1,0:T(8,128)(2,1)S(1)}, bf16[2,4,128,256]{3,2,1,0:T(8,128)(2,1)S(1)}, bf16[24,128,128]{2,1,0:T(8,128)(2,1)S(1)}) custom-call(s32[3,1,24]{2,1,0:T(1,128)} %bitcast.6, s32[1,1,3]{2,1,0:T(1,128)} %bitcast.11, bf16[4,2,128,256]{3,2,1,0:T(8,128)(2,1)} %bitcast.5, ...), custom_call_target="tpu_custom_call" | custom-call | flops 268435456 | bytes 1048576 | tf_op jit(solution)/shard_map/pallas_call | solution.py:269
  2.8 2.0 %shard_map.70 = (f32[512,256]{1,0:T(8,128)S(1)}, bf16[2,512,512]{2,1,0:T(8,128)(2,1)S(1)}, bf16[512,256]{1,0:T(8,128)(2,1)S(1)}, bf16[2,24,128,128]{3,2,1,0:T(8,128)(2,1)S(1)}) custom-call(s32[3,1,24]{2,1,0:T(1,128)} %bitcast.7, s32[1,1,3]{2,1,0:T(1,128)} %bitcast.12, bf16[2,4,128,256]{3,2,1,0:T(8,128)(2,1)S(1)} %get-tuple-element.34.refs_2_.users_ref, ...), custom_call_target="tpu_custom_call" | custom-call | flops 536870912 | bytes 2097152 | tf_op jit(solution)/shard_map/pallas_call | solution.py:269
  4.8 4.4 %collective-permute-start.4 = (f32[512,256]{1,0:T(8,128)S(1)}, f32[512,256]{1,0:T(8,128)S(1)}, u32[]{:S(2)}, u32[]{:S(2)}) collective-permute-start(f32[512,256]{1,0:T(8,128)S(1)} %get-tuple-element.42), channel_id=1, source_target_pairs={{0,8},{8,16},{16,24},{24,32},{32,40},{40,48},{48,56},{56,64},{64,7... | collective-permute-start | bytes 1572872 | tf_op jit(solution)/shard_map/ppermute | solution.py:39
  9.1 3.6 %collective-permute-start.2 = (f32[256,256]{1,0:T(8,128)S(1)}, f32[256,256]{1,0:T(8,128)S(1)}, u32[]{:S(2)}, u32[]{:S(2)}) collective-permute-start(f32[256,256]{1,0:T(8,128)S(1)} %get-tuple-element.39), channel_id=1, source_target_pairs={{0,8},{8,16},{16,24},{24,32},{32,40},{40,48},{48,56},{56,64},{64,7... | collective-permute-start | bytes 786440 | tf_op jit(solution)/shard_map/ppermute | solution.py:39
  12.7 1.5 %shard_map.71.spread_ref = bf16[2,512,1024]{2,1,0:T(8,128)(2,1)S(1)} custom-call(s32[3,1,24]{2,1,0:T(1,128)} %bitcast.8, s32[1,1,3]{2,1,0:T(1,128)} %bitcast.13, bf16[2,24,128,128]{3,2,1,0:T(8,128)(2,1)S(1)} %get-tuple-element.37.rating_ref), custom_call_target="tpu_custom_call" | custom-call | flops 134217728 | bytes 524288 | tf_op jit(solution)/shard_map/pallas_call | solution.py:269
  14.2 16.6 %collective-permute-done.4.panel_ref = f32[512,256]{1,0:T(8,128)S(1)} collective-permute-done((f32[512,256]{1,0:T(8,128)S(1)}, f32[512,256]{1,0:T(8,128)S(1)}, u32[]{:S(2)}, u32[]{:S(2)}) %collective-permute-start.4) | collective-permute-done | bytes 524320 | tf_op jit(solution)/shard_map/ppermute | solution.py:39
  30.8 0.9 %shard_map.76 = (f32[512,256]{1,0:T(8,128)S(1)}, bf16[2,512,512]{2,1,0:T(8,128)(2,1)S(1)}, bf16[512,256]{1,0:T(8,128)(2,1)S(1)}) custom-call(bf16[2,4,128,256]{3,2,1,0:T(8,128)(2,1)S(1)} %get-tuple-element.34.refs_2_.users_ref, f32[512,256]{1,0:T(8,128)S(1)} %collective-permute-done.4.panel_ref, bf16[2,512,1024]{2,1,0:T(8,128)(2,1)S(1)} %shard_map.71.spread_ref), custom_call_target="tpu_custom_call" | custom-call | flops 536870912 | bytes 2097152 | tf_op jit(solution)/shard_map/pallas_call | solution.py:269
  31.7 1.9 %collective-permute-start.5 = (f32[512,256]{1,0:T(8,128)S(1)}, f32[512,256]{1,0:T(8,128)S(1)}, u32[]{:S(2)}, u32[]{:S(2)}) collective-permute-start(f32[512,256]{1,0:T(8,128)S(1)} %get-tuple-element.43), channel_id=1, source_target_pairs={{0,8},{8,16},{16,24},{24,32},{32,40},{40,48},{48,56},{56,64},{64,7... | collective-permute-start | bytes 1572872 | tf_op jit(solution)/shard_map/ppermute | solution.py:39
  33.6 1.8 %shard_map.69 = (f32[256,256]{1,0:T(8,128)S(1)}, bf16[2,512,256]{2,1,0:T(8,128)(2,1)S(1)}, bf16[256,256]{1,0:T(8,128)(2,1)S(1)}) custom-call(s32[3,1,24]{2,1,0:T(1,128)} %bitcast.9, s32[1,1,3]{2,1,0:T(1,128)} %bitcast.14, bf16[2,4,128,256]{3,2,1,0:T(8,128)(2,1)S(1)} %get-tuple-element.34.refs_2_.users_ref, f32[1024,256]{1,0:T(8,128)} %refs_3_.3, ...), custom_call_target="tpu_custom_call" | custom-call | flops 268435456 | bytes 1048576 | tf_op jit(solution)/shard_map/pallas_call | solution.py:269
  35.4 1.9 %collective-permute-start = (f32[256,256]{1,0:T(8,128)S(1)}, f32[256,256]{1,0:T(8,128)S(1)}, u32[]{:S(2)}, u32[]{:S(2)}) collective-permute-start(f32[256,256]{1,0:T(8,128)S(1)} %get-tuple-element.36), channel_id=1, source_target_pairs={{0,8},{8,16},{16,24},{24,32},{32,40},{40,48},{48,56},{56,64},{64,7... | collective-permute-start | bytes 786440 | tf_op jit(solution)/shard_map/ppermute | solution.py:39
  37.3 0.0 collective-permute-done.2.panel_ref
  37.3 0.8 shard_map.74
  38.1 1.9 %collective-permute-start.3 = (f32[256,256]{1,0:T(8,128)S(1)}, f32[256,256]{1,0:T(8,128)S(1)}, u32[]{:S(2)}, u32[]{:S(2)}) collective-permute-start(f32[256,256]{1,0:T(8,128)S(1)} %get-tuple-element.40), channel_id=1, source_target_pairs={{0,8},{8,16},{16,24},{24,32},{32,40},{40,48},{48,56},{56,64},{64,7... | collective-permute-start | bytes 786440 | tf_op jit(solution)/shard_map/ppermute | solution.py:39
  40.0 13.9 %collective-permute-done.panel_ref = f32[256,256]{1,0:T(8,128)S(1)} collective-permute-done((f32[256,256]{1,0:T(8,128)S(1)}, f32[256,256]{1,0:T(8,128)S(1)}, u32[]{:S(2)}, u32[]{:S(2)}) %collective-permute-start) | collective-permute-done | bytes 262176 | tf_op jit(solution)/shard_map/ppermute | solution.py:39
  53.9 0.8 shard_map.72
  54.7 1.9 %collective-permute-start.1 = (f32[256,256]{1,0:T(8,128)S(1)}, f32[256,256]{1,0:T(8,128)S(1)}, u32[]{:S(2)}, u32[]{:S(2)}) collective-permute-start(f32[256,256]{1,0:T(8,128)S(1)} %get-tuple-element.38), channel_id=1, source_target_pairs={{0,8},{8,16},{16,24},{24,32},{32,40},{40,48},{48,56},{56,64},{64,7... | collective-permute-start | bytes 786440 | tf_op jit(solution)/shard_map/ppermute | solution.py:39
  56.6 1.5 %shard_map.73.spread_ref = bf16[2,512,1024]{2,1,0:T(8,128)(2,1)S(1)} custom-call(s32[3,1,24]{2,1,0:T(1,128)} %bitcast.10, s32[1,1,3]{2,1,0:T(1,128)} %bitcast.15, bf16[2,24,128,128]{3,2,1,0:T(8,128)(2,1)S(1)} %get-tuple-element.37.rating_ref), custom_call_target="tpu_custom_call" | custom-call | flops 134217728 | bytes 524288 | tf_op jit(solution)/shard_map/pallas_call | solution.py:269
  58.1 0.7 shard_map.78.refs_6_
  58.8 0.7 collective-permute-done.3.panel_ref
  59.5 0.8 shard_map.75
  60.3 0.7 shard_map.79.refs_4_
  61.0 0.0 collective-permute-done.5.panel_ref
  61.0 0.9 %shard_map.77 = (f32[512,256]{1,0:T(8,128)S(1)}, bf16[2,512,512]{2,1,0:T(8,128)(2,1)S(1)}, bf16[512,256]{1,0:T(8,128)(2,1)S(1)}) custom-call(bf16[2,4,128,256]{3,2,1,0:T(8,128)(2,1)S(1)} %get-tuple-element.34.refs_2_.users_ref, f32[512,256]{1,0:T(8,128)S(1)} %collective-permute-done.5.panel_ref, bf16[2,512,1024]{2,1,0:T(8,128)(2,1)S(1)} %shard_map.73.spread_ref), custom_call_target="tpu_custom_call" | custom-call | flops 536870912 | bytes 2097152 | tf_op jit(solution)/shard_map/pallas_call | solution.py:269
  61.9 0.6 shard_map.80.total_ref
  62.5 2.6 %collective-permute-done.1.panel_ref = f32[256,256]{1,0:T(8,128)S(1)} collective-permute-done((f32[256,256]{1,0:T(8,128)S(1)}, f32[256,256]{1,0:T(8,128)S(1)}, u32[]{:S(2)}, u32[]{:S(2)}) %collective-permute-start.1) | collective-permute-done | bytes 262176 | tf_op jit(solution)/shard_map/ppermute | solution.py:39
  65.1 0.6 shard_map.81
  65.7 8.6 %collective-permute-start.6 = (f32[512,256]{1,0:T(8,128)S(1)}, f32[512,256]{1,0:T(8,128)S(1)}, u32[]{:S(2)}, u32[]{:S(2)}) collective-permute-start(f32[512,256]{1,0:T(8,128)S(1)} %get-tuple-element.65), channel_id=1, source_target_pairs={{0,1},{1,0},{2,3},{3,2},{4,5},{5,4},{6,7},{7,6},{8,9},{9,8},{10,11... | collective-permute-start | bytes 1572872 | tf_op jit(solution)/shard_map/ppermute | solution.py:360
  74.3 1.4 %shard_map.82 = (f32[512,256]{1,0:T(8,128)S(1)}, f32[1024,256]{1,0:T(8,128)}) custom-call(bf16[2,4,128,256]{3,2,1,0:T(8,128)(2,1)S(1)} %get-tuple-element.34.refs_2_.users_ref, f32[256,256]{1,0:T(8,128)S(1)} %collective-permute-done.1.panel_ref, bf16[2,512,256]{2,1,0:T(8,128)(2,1)S(1)} %get-tuple-element.59.residual_ref, ...), custom_call_target="tpu_custom_call" | custom-call | flops 268435456 | bytes 1048576 | tf_op jit(solution)/shard_map/pallas_call | solution.py:269
  75.7 0.1 collective-permute-done.6
  75.8 0.1 add.3
  75.9 12.4 %all_to_all.5.shares_ref = f32[4,128,256]{2,1,0:T(8,128)S(1)} all-to-all(f32[4,128,256]{2,1,0:T(8,128)S(1)} %bitcast.4), channel_id=1, replica_groups={{0,2,4,6},{1,3,5,7},{8,10,12,14},{9,11,13,15},{16,18,20,22},{17,19,21,2..., dimensions={0} | all-to-all | bytes 1048576 | tf_op jit(solution)/shard_map/all_to_all | solution.py:367
  88.3 0.7 shard_map.83
Async XLA Ops:
  4.8 26.0 %collective-permute-start.4 = (f32[512,256]{1,0:T(8,128)S(1)}, f32[512,256]{1,0:T(8,128)S(1)}, u32[]{:S(2)}, u32[]{:S(2)}) collective-permute-start(f32[512,256]{1,0:T(8,128)S(1)} %get-tuple-element.42), channel_id=1, source_target_pairs={{0,8},{8,16},{16,24},{24,32},{32,40},{40,48},{48,56},{56,64},{64,7... | collective-permute-start | bytes 1572872 | tf_op jit(solution)/shard_map/ppermute | solution.py:39
  9.1 28.2 %collective-permute-start.2 = (f32[256,256]{1,0:T(8,128)S(1)}, f32[256,256]{1,0:T(8,128)S(1)}, u32[]{:S(2)}, u32[]{:S(2)}) collective-permute-start(f32[256,256]{1,0:T(8,128)S(1)} %get-tuple-element.39), channel_id=1, source_target_pairs={{0,8},{8,16},{16,24},{24,32},{32,40},{40,48},{48,56},{56,64},{64,7... | collective-permute-start | bytes 786440 | tf_op jit(solution)/shard_map/ppermute | solution.py:39
  31.7 29.3 %collective-permute-start.5 = (f32[512,256]{1,0:T(8,128)S(1)}, f32[512,256]{1,0:T(8,128)S(1)}, u32[]{:S(2)}, u32[]{:S(2)}) collective-permute-start(f32[512,256]{1,0:T(8,128)S(1)} %get-tuple-element.43), channel_id=1, source_target_pairs={{0,8},{8,16},{16,24},{24,32},{32,40},{40,48},{48,56},{56,64},{64,7... | collective-permute-start | bytes 1572872 | tf_op jit(solution)/shard_map/ppermute | solution.py:39
  35.4 18.5 %collective-permute-start = (f32[256,256]{1,0:T(8,128)S(1)}, f32[256,256]{1,0:T(8,128)S(1)}, u32[]{:S(2)}, u32[]{:S(2)}) collective-permute-start(f32[256,256]{1,0:T(8,128)S(1)} %get-tuple-element.36), channel_id=1, source_target_pairs={{0,8},{8,16},{16,24},{24,32},{32,40},{40,48},{48,56},{56,64},{64,7... | collective-permute-start | bytes 786440 | tf_op jit(solution)/shard_map/ppermute | solution.py:39
  38.1 21.4 %collective-permute-start.3 = (f32[256,256]{1,0:T(8,128)S(1)}, f32[256,256]{1,0:T(8,128)S(1)}, u32[]{:S(2)}, u32[]{:S(2)}) collective-permute-start(f32[256,256]{1,0:T(8,128)S(1)} %get-tuple-element.40), channel_id=1, source_target_pairs={{0,8},{8,16},{16,24},{24,32},{32,40},{40,48},{48,56},{56,64},{64,7... | collective-permute-start | bytes 786440 | tf_op jit(solution)/shard_map/ppermute | solution.py:39
  54.7 10.4 %collective-permute-start.1 = (f32[256,256]{1,0:T(8,128)S(1)}, f32[256,256]{1,0:T(8,128)S(1)}, u32[]{:S(2)}, u32[]{:S(2)}) collective-permute-start(f32[256,256]{1,0:T(8,128)S(1)} %get-tuple-element.38), channel_id=1, source_target_pairs={{0,8},{8,16},{16,24},{24,32},{32,40},{40,48},{48,56},{56,64},{64,7... | collective-permute-start | bytes 786440 | tf_op jit(solution)/shard_map/ppermute | solution.py:39
  65.7 10.1 %collective-permute-start.6 = (f32[512,256]{1,0:T(8,128)S(1)}, f32[512,256]{1,0:T(8,128)S(1)}, u32[]{:S(2)}, u32[]{:S(2)}) collective-permute-start(f32[512,256]{1,0:T(8,128)S(1)} %get-tuple-element.65), channel_id=1, source_target_pairs={{0,1},{1,0},{2,3},{3,2},{4,5},{5,4},{6,7},{7,6},{8,9},{9,8},{10,11... | collective-permute-start | bytes 1572872 | tf_op jit(solution)/shard_map/ppermute | solution.py:360
